TPU v7x, 32 devices: a whole 2x2x4 slice. The times are simulated.
32 devices in a mesh: lat: 4 (over z), lev: 8 (over y, x, core).
Axes of the slice: x: 2, y: 2, z: 4, core: 2. Of those that a mesh axis runs over, the one named last changes fastest.
Arguments:
- spec_in: bfloat16 [8, 2, 8, 2560], P('lat', None, None, 'lev'), may hold values from -6 to 6
- legendre: bfloat16 [8, 2560, 2560], P('lat', 'lev'), may hold values from -0.125 to 0.125
- pattern: int32 [8, 20, 20], P('lat'), may hold values from 0 to 1, as said below
- deal_list: int32 [8], replicated, may hold values from 0 to 2559, as said below
- circle_lengths: int32 [2560], replicated, may hold values from 12 to 10256, as said below
- mixing: bfloat16 [8, 8], replicated, may hold values from -2 to 2
Outputs:
- spec_out: float32 [8, 2, 8, 2560], P('lat', None, None, 'lev')
Inputs may be any that keep to these rules, and one draw needn't show every extreme that they name: `deal_list`: distinct wavenumbers; 0 and 2559 are always among them. pattern[m, a, b] is 1 exactly when b * 128 <= 2559 - deal_list[m] and a >= (deal_list[m] * 20) // 5120, else 0. `circle_lengths`: multiples of 4; row j holds a value between 20 + 4 j - 4 (j // 2 + 2) and 20 + 4 j, and the last row exactly 20 + 4 (2559).
All inputs are finite; a program needn't handle non-finite values.
Results may differ from a plain program's by a relative error of at most 0.0026.
Values may be sent and summed in bfloat16 or wider, within the bound.
A program may use at most 64 MiB of HBM per device.

v0:
```python
import functools
import math

import jax
import jax.numpy as jnp
from jax import lax
from jax.experimental import pallas as pl
from jax.experimental.pallas import tpu as pltpu
from jax.sharding import PartitionSpec as P

BLK = 128
TILES = 2
STREAMS = 12


def row_kernel(
    packed, lengths, deal, fourier_ref, mixing_ref, table_ref, weight_ref, out_ref, left, total
):
    lat_count, count, block_width = fourier_ref.shape
    rows = table_ref.shape[0]
    waves = table_ref.shape[1] // 4
    fields = mixing_ref.shape[0]
    hf, width = 2 * fields, 2 * waves
    pack = rows // count
    part_span = block_width // pack
    lanes = lat_count * part_span
    span = TILES * BLK
    devices = lat_count * lax.axis_size("lev")
    device = lax.axis_index("lev") * lat_count + lax.axis_index("lat")
    lane_of = lax.broadcasted_iota(jnp.int32, (1, lanes), 1)
    first_lane = jnp.zeros((1, lanes), jnp.int32)
    kind = lax.broadcasted_iota(jnp.int32, (1, width), 1)
    both = jnp.zeros((1, width), jnp.float32)
    for wave in range(waves):
        cut = deal[wave] * (pack * packed // BLK) // (2 * pack * packed)
        first_lane = jnp.where(lane_of // (4 * fields) == wave, cut, first_lane)
        odd = (1 - 2 * (deal[wave] % 2)).astype(jnp.float32)
        both = jnp.where(kind % waves == wave, odd, both)
    flip = jnp.where(kind < waves, 1.0, -1.0).astype(jnp.float32)
    signs = [jnp.ones_like(both), flip, both, both * flip]
    blocks = [fourier_ref[side].astype(jnp.float32) for side in range(lat_count)]
    values = jnp.concatenate(
        [
            jnp.concatenate(
                [block[:, part * part_span : (part + 1) * part_span] for block in blocks], axis=1
            )
            for part in range(pack)
        ],
        axis=0,
    )
    row_in = lax.broadcasted_iota(jnp.int32, (count, 1), 0) * devices + device
    live = jnp.concatenate(
        [
            jnp.where((row_in + part * packed) // BLK >= first_lane, 1.0, 0.0)
            for part in range(pack)
        ],
        axis=0,
    ).astype(jnp.float32)
    values = (values * live).astype(jnp.bfloat16)
    keep_lane = lane_of // (2 * fields) % 2 * fields + lane_of % fields
    keep = (
        lax.broadcasted_iota(jnp.int32, (hf, lanes), 0) == keep_lane
    ).astype(jnp.float32)
    down = lax.broadcasted_iota(jnp.int32, (lanes, width), 0)
    gather = (
        down // fields % 2 * waves + down // (4 * fields)
        == lax.broadcasted_iota(jnp.int32, (lanes, width), 1)
    ).astype(jnp.float32).astype(jnp.bfloat16)
    pick = (
        lax.broadcasted_iota(jnp.int32, (BLK, fields), 0) % fields
        == lax.broadcasted_iota(jnp.int32, (BLK, fields), 1)
    ).astype(jnp.float32).astype(jnp.bfloat16)
    across = (((1,), (1,)), ((), ()))
    half_mixer = lax.dot_general(
        pick, mixing_ref[...], across, preferred_element_type=jnp.float32
    ).astype(jnp.bfloat16)
    mixer = lax.dot_general(half_mixer, pick, across, preferred_element_type=jnp.float32)
    same = (
        lax.broadcasted_iota(jnp.int32, (BLK, BLK), 0) // fields
        == lax.broadcasted_iota(jnp.int32, (BLK, BLK), 1) // fields
    )
    mixer = jnp.where(same, mixer, 0.0).astype(jnp.bfloat16)
    mixed = jnp.concatenate(
        [
            jnp.dot(values[:, at : at + BLK], mixer, preferred_element_type=jnp.float32)
            for at in range(0, lanes, BLK)
        ],
        axis=1,
    )
    scale = (2.0 * waves) ** (-0.5)

    def fold(source):
        spread = (source[:, None, :] * keep[None, :, :]).reshape(rows * hf, lanes)
        return scale * jnp.dot(
            spread.astype(jnp.bfloat16), gather, preferred_element_type=jnp.float32
        )

    high = mixed.astype(jnp.bfloat16).astype(jnp.float32)
    straight, mix_high, mix_low = fold(values.astype(jnp.float32)), fold(high), fold(mixed - high)
    pairs = (
        jnp.concatenate([straight, jnp.zeros_like(straight)], axis=1),
        jnp.concatenate([mix_high, mix_low], axis=1),
    )
    for part, source in enumerate(pairs):
        for image in range(4):
            sign = signs[image]
            signed = source * jnp.concatenate([sign, sign], axis=1)
            at = (2 * image + part) * hf
            left[:rows, at : at + hf, :] = signed.reshape(rows, hf, 2 * width).astype(jnp.bfloat16)

    lane = lax.broadcasted_iota(jnp.int32, (1, span), 1)

    def proceed(state):
        return state[1]

    def advance(state):
        following, _, streams = state
        stages = []
        for row, index, cos_held, sin_held, sums in streams:
            quarter = lengths[jnp.minimum(row, rows - 1)] // 4
            at = jnp.minimum(row, rows - 1)
            fresh = index == 0
            cos_now = jnp.where(fresh, table_ref[at, 0:waves, :], cos_held)
            sin_now = jnp.where(fresh, table_ref[at, waves : 2 * waves, :], sin_held)
            step_cos = table_ref[at, 2 * waves : 3 * waves, :]
            step_sin = table_ref[at, 3 * waves : 4 * waves, :]
            cosines, sines = [], []
            for _ in range(TILES):
                cosines.append(cos_now)
                sines.append(-sin_now)
                cos_now, sin_now = (
                    cos_now * step_cos - sin_now * step_sin,
                    sin_now * step_cos + cos_now * step_sin,
                )
            phases = jnp.concatenate(
                [jnp.concatenate(cosines, axis=1), jnp.concatenate(sines, axis=1)], axis=0
            ).astype(jnp.bfloat16)
            stages.append((at, quarter, fresh, cos_now, sin_now, phases))
        grids = [
            jnp.dot(
                left[stage[0]],
                jnp.concatenate([stage[5], stage[5]], axis=0),
                preferred_element_type=jnp.float32,
            )
            for stage in stages
        ]
        added = []
        for stream, stage, grid in zip(streams, stages, grids):
            quarter, phases = stage[1], stage[5]
            position = lane + stream[1] * span
            share = jnp.where(
                (position == 0) | (position == quarter),
                0.5,
                jnp.where(position < quarter, 1.0, 0.0),
            ).astype(jnp.float32)
            columns = []
            for image in range(4):
                at = 2 * image * hf
                columns.append(
                    ((grid[at : at + hf] + jnp.tanh(grid[at + hf : at + 2 * hf])) * share).astype(
                        jnp.bfloat16
                    )
                )
            added.append(
                lax.dot_general(
                    jnp.concatenate(columns, axis=0),
                    phases,
                    (((1,), (1,)), ((), ())),
                    preferred_element_type=jnp.float32,
                )
            )
        later = []
        busy = jnp.bool_(False)
        for stream, stage, extra in zip(streams, stages, added):
            row, index, _, _, sums = stream
            sums = jnp.where(stage[2], 0.0, sums) + extra
            whole = sum(
                sums[image * hf : (image + 1) * hf] * signs[image]
                for image in range(4)
            )
            total[row] = whole
            done = (index + 1) * span > stage[1]
            idle = row >= rows
            taken = jnp.logical_and(done, jnp.logical_not(idle))
            row = jnp.where(taken, following, row)
            following = following - taken.astype(jnp.int32)
            row = jnp.where(row < 0, rows, row)
            index = jnp.where(done, 0, index + 1)
            busy = jnp.logical_or(busy, row < rows)
            later.append((row, index, stage[3], stage[4], sums))
        return following, busy, tuple(later)

    held = jnp.zeros((waves, BLK), jnp.float32)
    streams = tuple(
        (
            jnp.int32(rows - 1 - stream if stream < rows else rows),
            jnp.int32(0),
            held,
            held,
            jnp.zeros((4 * hf, width), jnp.float32),
        )
        for stream in range(STREAMS)
    )
    lax.while_loop(
        proceed, advance, (jnp.int32(rows - 1 - STREAMS), jnp.bool_(True), streams)
    )
    spread = lax.dot_general(
        (total[:rows] * weight_ref[...]).reshape(rows * hf, width).astype(jnp.bfloat16),
        gather,
        (((1,), (1,)), ((), ())),
        preferred_element_type=jnp.float32,
    )
    summed = jnp.sum(spread.reshape(rows, hf, lanes) * keep[None, :, :], axis=1)
    summed = summed * live
    for side in range(lat_count):
        out_ref[side] = jnp.concatenate(
            [
                summed[
                    part * count : (part + 1) * count, side * part_span : (side + 1) * part_span
                ]
                for part in range(pack)
            ],
            axis=1,
        ).astype(jnp.bfloat16)


def wave_tables(deal_list, lengths):
    rows, waves = lengths.shape[0], deal_list.shape[0]
    length = lengths.astype(jnp.float32)[:, None, None]
    wave = deal_list.astype(jnp.float32)[None, :, None]

    def angle_of(position):
        product = wave * position
        turned = product - jnp.floor(product / length) * length
        return turned * (2.0 * math.pi) / length

    inner = angle_of(jnp.arange(BLK, dtype=jnp.float32)[None, None, :])
    step = angle_of(jnp.full((1, 1, 1), float(BLK), jnp.float32))
    shape = (rows, waves, BLK)
    return jnp.concatenate(
        [
            jnp.cos(inner),
            jnp.sin(inner),
            jnp.broadcast_to(jnp.cos(step), shape),
            jnp.broadcast_to(jnp.sin(step), shape),
        ],
        axis=1,
    )


def rows_step(fourier, lengths, row_ids, deal_list, mixing, half_lat):
    fields, waves, rows = mixing.shape[0], deal_list.shape[0], row_ids.shape[0]
    hf, width = 2 * fields, 2 * waves
    pack = rows // fourier.shape[1]
    tables = wave_tables(deal_list, lengths)
    weight = jnp.sin(math.pi * (row_ids.astype(jnp.float32) + 0.5) / (2 * half_lat)) / jnp.sqrt(
        lengths.astype(jnp.float32)
    )
    vmem = pl.BlockSpec(memory_space=pltpu.VMEM)
    smem = pl.BlockSpec(memory_space=pltpu.SMEM)
    return pl.pallas_call(
        functools.partial(row_kernel, half_lat // pack),
        out_shape=jax.ShapeDtypeStruct(fourier.shape, jnp.bfloat16),
        in_specs=[smem, smem] + [vmem] * 4,
        out_specs=vmem,
        scratch_shapes=[
            pltpu.VMEM((rows, 8 * hf, 2 * width), jnp.bfloat16),
            pltpu.VMEM((rows + 1, hf, width), jnp.float32),
        ],
    )(lengths, deal_list, fourier, mixing, tables, weight[:, None, None])


def column_masks(pattern_ref, local_cols):
    slots, blocks_down, blocks = pattern_ref.shape
    column = lax.broadcasted_iota(jnp.int32, (1, local_cols), 1)
    column = column + lax.axis_index("lev") * local_cols
    odd = (1 - 2 * (column % 2)).astype(jnp.float32)
    masks = []
    for slot in range(slots):
        mask = jnp.zeros((1, local_cols), jnp.float32)
        for block in range(blocks):
            kept = pattern_ref[slot, blocks_down - 1, block].astype(jnp.float32)
            mask = jnp.where(column // BLK == block, kept, mask)
        masks.append(mask)
    return odd, masks


def peers_of(axis):
    count = lax.axis_size(axis)
    return [lax.rem(lax.axis_index(axis) + off, count) for off in range(1, count)]


def greet():
    expect(hail())


def expect(total):
    pl.semaphore_wait(pltpu.get_barrier_semaphore(), total)


def hail():
    barrier = pltpu.get_barrier_semaphore()
    total = 0
    for axis in ("lat", "lev"):
        for peer in peers_of(axis):
            pl.semaphore_signal(
                barrier, inc=1, device_id={axis: peer}, device_id_type=pl.DeviceIdType.MESH
            )
            total += 1
    return total


def send(axis, sources, target, sems):
    copies = []
    for step, peer in enumerate(peers_of(axis)):
        copy = pltpu.make_async_remote_copy(
            src_ref=sources(peer),
            dst_ref=target,
            send_sem=sems.at[0, step],
            recv_sem=sems.at[1, step],
            device_id={axis: peer},
            device_id_type=pl.DeviceIdType.MESH,
        )
        copy.start()
        copies.append(copy)
    return copies


def inward_kernel(pack, pattern_ref, spec_ref, legendre_ref, out_ref, turned, leaving, arriving, summed, landed,
                  lev_sems, lat_sems):
    slots, _, half_lat = legendre_ref.shape
    lev_count, lat_count, count, width = leaving.shape
    devices = lev_count * lat_count
    lev_index, lat_index = lax.axis_index("lev"), lax.axis_index("lat")
    packed = half_lat // pack
    greetings = hail()
    odd, masks = column_masks(pattern_ref, legendre_ref.shape[1])
    sums = []
    for slot in range(slots):
        kept = jnp.concatenate([spec_ref[slot, 0], spec_ref[slot, 1]], axis=0).astype(jnp.float32)
        kept = kept * masks[slot]
        sums.append(
            jnp.dot(
                jnp.concatenate([kept, kept * odd], axis=0).astype(jnp.bfloat16),
                legendre_ref[slot],
                preferred_element_type=jnp.float32,
            )
        )
    for block in range(packed // BLK):
        piece = jnp.concatenate(
            [
                value[:, part * packed + block * BLK : part * packed + (block + 1) * BLK]
                for part in range(pack)
                for value in sums
            ],
            axis=0,
        )
        turned[:, block * BLK : (block + 1) * BLK, :] = jnp.stack(
            [piece[at : at + BLK].T for at in range(0, width, BLK)]
        )
    for device in range(devices):
        for at in range(width // BLK):
            leaving[device // lat_count, device % lat_count, :, at * BLK : (at + 1) * BLK] = (
                turned[at, pl.ds(device, count, stride=devices), :].astype(jnp.bfloat16)
            )
    expect(greetings)
    copies = send("lev", lambda peer: leaving.at[peer], arriving.at[lev_index], lev_sems)
    mine = lev_index * lat_count
    total = jnp.stack(
        [
            jnp.concatenate(
                [
                    turned[at, pl.ds(mine + side, count, stride=devices), :]
                    for at in range(width // BLK)
                ],
                axis=1,
            )
            for side in range(lat_count)
        ]
    )
    for copy, peer in zip(copies, [lax.rem(lev_index + lev_count - off, lev_count) for off in range(1, lev_count)]):
        copy.wait_recv()
        total = total + arriving[peer].astype(jnp.float32)
    summed[...] = total.astype(jnp.bfloat16)
    crossing = send("lat", lambda peer: summed.at[peer], landed.at[lat_index], lat_sems)
    out_ref[lat_index] = summed[lat_index]
    for copy, peer in zip(crossing, [lax.rem(lat_index + lat_count - off, lat_count) for off in range(1, lat_count)]):
        copy.wait_recv()
        out_ref[peer] = landed[peer]
    for copy in copies + crossing:
        copy.wait_send()


def outward_kernel(pack, fields, pattern_ref, rows_ref, legendre_ref, out_ref, held, landed, gathered, turned,
                   lev_sems, lat_sems, load_sem):
    slots, local_cols, half_lat = held.shape
    lev_count, lat_count, count, width = gathered.shape
    devices = lev_count * lat_count
    lev_index, lat_index = lax.axis_index("lev"), lax.axis_index("lat")
    packed = half_lat // pack
    part_width = 4 * fields
    load = pltpu.make_async_copy(legendre_ref, held, load_sem)
    load.start()
    greet()
    crossing = send("lat", lambda peer: rows_ref.at[peer], landed.at[lat_index], lat_sems)
    landed[lat_index] = rows_ref[lat_index]
    for copy in crossing:
        copy.wait_recv()
    copies = send("lev", lambda peer: landed, gathered.at[lev_index], lev_sems)
    gathered[lev_index] = landed[...]
    for copy in copies:
        copy.wait_recv()
    for device in range(devices):
        block = gathered[device // lat_count, device % lat_count].astype(jnp.float32)
        for at in range(width // BLK):
            turned[at, pl.ds(device, count, stride=devices), :] = block[:, at * BLK : (at + 1) * BLK]
    load.wait()
    odd, masks = column_masks(pattern_ref, local_cols)
    sides = [turned[at].astype(jnp.bfloat16) for at in range(width // BLK)]
    for slot in range(slots):
        total = None
        for part in range(pack):
            at = part * slots * part_width + slot * part_width
            value = jnp.dot(
                held[slot, :, part * packed : (part + 1) * packed],
                sides[at // BLK],
                preferred_element_type=jnp.float32,
            )[:, at % BLK : at % BLK + part_width]
            total = value if total is None else total + value
        flat = total.T
        joined = flat[: 2 * fields] + odd * flat[2 * fields :]
        out_ref[slot] = joined * masks[slot]
    for copy in copies + crossing:
        copy.wait_send()


def local(spec_in, legendre, pattern, deal_list, circle_lengths, mixing):
    lat_index = lax.axis_index("lat")
    lev_index = lax.axis_index("lev")
    lat_count = lax.axis_size("lat")
    lev_count = lax.axis_size("lev")
    slots, local_cols, half_lat = legendre.shape
    fields = spec_in.shape[2]
    devices = lat_count * lev_count
    rows = half_lat // devices
    span = 4 * slots * fields
    pack = max(1, BLK // span)
    count, width = rows // pack, span * pack
    vmem = pl.BlockSpec(memory_space=pltpu.VMEM)
    block_shape = (lat_count, count, width)
    sems = [
        pltpu.SemaphoreType.DMA((2, lev_count)),
        pltpu.SemaphoreType.DMA((2, lat_count)),
    ]
    turned = pltpu.VMEM((width // BLK, half_lat // pack, BLK), jnp.float32)
    fourier = pl.pallas_call(
        functools.partial(inward_kernel, pack),
        out_shape=jax.ShapeDtypeStruct(block_shape, jnp.bfloat16),
        in_specs=[pl.BlockSpec(memory_space=pltpu.SMEM), vmem, vmem],
        out_specs=vmem,
        scratch_shapes=[
            turned,
            pltpu.VMEM((lev_count,) + block_shape, jnp.bfloat16),
            pltpu.VMEM((lev_count,) + block_shape, jnp.bfloat16),
            pltpu.VMEM(block_shape, jnp.bfloat16),
            pltpu.VMEM(block_shape, jnp.bfloat16),
        ]
        + sems,
        compiler_params=pltpu.CompilerParams(collective_id=0, has_side_effects=True),
    )(pattern, spec_in, legendre)
    row_ids = (
        jnp.arange(pack, dtype=jnp.int32)[:, None] * (half_lat // pack)
        + jnp.arange(count, dtype=jnp.int32)[None, :] * devices
        + (lev_index * lat_count + lat_index)
    ).reshape(rows)
    by_device = circle_lengths.reshape(rows, devices)
    chosen = jnp.arange(devices, dtype=jnp.int32)[None, :] == lev_index * lat_count + lat_index
    lengths = jnp.sum(jnp.where(chosen, by_device, 0), axis=1)
    leaving = rows_step(fourier, lengths, row_ids, deal_list, mixing, half_lat)
    product = pl.pallas_call(
        functools.partial(outward_kernel, pack, fields),
        out_shape=jax.ShapeDtypeStruct((slots, 2 * fields, local_cols), jnp.float32),
        in_specs=[
            pl.BlockSpec(memory_space=pltpu.SMEM),
            vmem,
            pl.BlockSpec(memory_space=pl.ANY),
        ],
        out_specs=vmem,
        scratch_shapes=[
            pltpu.VMEM(legendre.shape, jnp.bfloat16),
            pltpu.VMEM(block_shape, jnp.bfloat16),
            pltpu.VMEM((lev_count,) + block_shape, jnp.bfloat16),
            turned,
        ]
        + sems
        + [pltpu.SemaphoreType.DMA],
        compiler_params=pltpu.CompilerParams(collective_id=1, has_side_effects=True),
    )(pattern, leaving, legendre)
    return product.reshape(slots, 2, fields, local_cols)


def solution(mesh):
    return jax.shard_map(
        local,
        mesh=mesh,
        in_specs=(
            P("lat", None, None, "lev"),
            P("lat", "lev", None),
            P("lat", None, None),
            P(),
            P(),
            P(),
        ),
        out_specs=P("lat", None, None, "lev"),
        check_vma=False,
    )
```

profile of v0, /device:TPU:0, one launch (start us, length us, event | category | flops | bytes accessed | tf_op | source)
XLA Modules:
  0.0 57.2 jit_solution(2436505876136267609)
XLA Ops:
  0.0 0.8 %reshape.236 = s32[80,32]{1,0:T(8,128)S(1)} reshape(s32[2560]{0:T(1024)} %param.10) | data formatting | bytes 20480 | tf_op jit(solution)/shard_map/reshape | solution.py:476
  0.8 0.1 select_reduce_fusion.lengths
  0.9 0.0 copy-start.1
  0.9 0.7 %convert_element_type.28 = f32[8]{0:T(128)S(1)} convert(s32[8]{0:T(128)} %deal.1) | non-fusion elementwise | flops 8 | bytes 64 | tf_op jit(solution)/shard_map/convert_element_type | solution.py:230
  1.6 0.1 iota_multiply_fusion
  1.7 1.3 %fusion.5 = (f32[80,8,128]{2,1,0:T(8,128)S(1)}, f32[80,8,128]{2,1,0:T(8,128)S(1)}) fusion(f32[80]{0:T(128)S(1)} %convert_element_type.29, f32[8,128]{1,0:T(8,128)S(1)} %iota_multiply_fusion), kind=kLoop, calls=%fused_computation.7 | loop fusion | flops 491520 | bytes 659776 | tf_op jit(solution)/shard_map/cos | solution.py:242
  2.9 0.7 %broadcast_multiply_fusion = f32[8]{0:T(128)S(1)} fusion(s32[8]{0:T(128)} %deal.1), kind=kLoop, calls=%fused_computation.22 | loop fusion | flops 16 | bytes 64 | tf_op jit(solution)/shard_map/mul | solution.py:233
  3.6 0.1 fusion.11
  3.7 0.1 copy.16
  3.8 0.1 broadcast_in_dim.18
  4.0 0.1 copy.17
  4.0 0.1 broadcast_in_dim.19
  4.2 0.0 copy-start
  4.2 1.2 %pad_maximum_fusion.table_ref = f32[80,32,128]{2,1,0:T(8,128)} fusion(f32[80,8,128]{2,1,0:T(8,128)S(1)} %broadcast_in_dim.19, f32[80,8,128]{2,1,0:T(8,128)S(1)} %broadcast_in_dim.18, f32[80,8,128]{2,1,0:T(8,128)S(1)} %get-tuple-element.6, f32[80,8,128]{2,1,0:T(8,128)S(1)} %get-tuple-element.5), kind=kLoop, calls=%fused_computation | loop fusion | flops 983040 | bytes 2621440 | tf_op jit(solution)/shard_map/concatenate | solution.py:240
  5.4 0.1 multiply_sine_fusion
  5.5 0.1 reshape.240
  5.6 0.0 copy-done.1
  5.6 0.7 %copy.18.weight_ref = f32[80,1,1]{2,1,0:T(1,128)} copy(f32[80,1,1]{0,2,1:T(1,128)S(1)} %bitcast_multiply_fusion) | data formatting | bytes 640 | tf_op jit(solution)/shard_map/div | solution.py:256
  6.3 0.0 copy-done
  6.3 0.6 %copy.19.pattern_ref = s32[2,20,20]{2,1,0:T(8,128)} copy(s32[2,20,20]{2,0,1:T(2,128)S(1)} %copy-done) | data formatting | bytes 6400 | tf_op args[2]
  6.9 16.7 %shard_map.64.fourier_ref = bf16[4,40,128]{2,1,0:T(8,128)(2,1)} custom-call(s32[2,20,20]{2,1,0:T(8,128)} %copy.19.pattern_ref, bf16[2,2,8,320]{3,2,1,0:T(8,128)(2,1)} %spec_ref.1, bf16[2,320,2560]{2,1,0:T(8,128)(2,1)} %legendre_ref.3), custom_call_target="tpu_custom_call" | custom-call | tf_op jit(solution)/shard_map/pallas_call | solution.py:456
  23.6 18.0 %shard_map.65.rows_ref = bf16[4,40,128]{2,1,0:T(8,128)(2,1)} custom-call(s32[80]{0:T(128)} %copy-done.1, s32[8]{0:T(128)} %deal.1, bf16[4,40,128]{2,1,0:T(8,128)(2,1)} %shard_map.64.fourier_ref, bf16[8,8]{1,0:T(8,128)(2,1)} %mixing_ref.1, f32[80,32,128]{2,1,0:T(8,128)} %pad_maximum_fusion.table_ref, f32[80,1,1]{2,1,0:T(1,128)} %copy.18.weight_ref), custom_call_target="tpu_custom_call" | custom-call | tf_op jit(solution)/shard_map/pallas_call | solution.py:261
  41.6 14.2 %shard_map.66 = f32[2,16,320]{2,1,0:T(8,128)} custom-call(s32[2,20,20]{2,1,0:T(8,128)} %copy.19.pattern_ref, bf16[4,40,128]{2,1,0:T(8,128)(2,1)} %shard_map.65.rows_ref, bf16[2,320,2560]{2,1,0:T(8,128)(2,1)} %legendre_ref.3), custom_call_target="tpu_custom_call" | custom-call | tf_op jit(solution)/shard_map/pallas_call | solution.py:480
  55.7 1.4 %copy.21 = f32[2,2,8,320]{3,2,1,0:T(8,128)} copy(f32[2,2,8,320]{3,2,1,0:T(8,128)} %bitcast.3) | data formatting | bytes 81920
  (5 shorter events, 0.0 us)
Async XLA Ops:
  0.9 4.7 %copy-start.1 = (s32[80]{0:T(128)}, s32[80]{0:T(128)S(1)}, u32[]{:S(2)}) copy-start(s32[80]{0:T(128)S(1)} %select_reduce_fusion.lengths) | copy-start | bytes 964
  4.2 2.1 %copy-start = (s32[2,20,20]{2,0,1:T(2,128)S(1)}, s32[2,20,20]{2,0,1:T(2,128)}, u32[]{:S(2)}) copy-start(s32[2,20,20]{2,0,1:T(2,128)} %param.8) | copy-start | bytes 9604
where the time goes:
time: 57.5 us; the launch traced here: 57.2 us
  Pallas kernels  48.8 us (85%)
  other arithmetic  4.18 us (7%)
  local copies, waits for them, and re-layouts  4.09 us (7%)
    pallas_call x1, Pallas kernels, rows_step(): pl.pallas_call(functools.partial(row_kernel, half_lat // pack), out_shape...  18 us
    pallas_call x1, Pallas kernels, local(): pl.pallas_call(functools.partial(inward_kernel, pack), out_shape=jax.Shap...  16.7 us
    pallas_call x1, Pallas kernels, local(): pl.pallas_call(functools.partial(outward_kernel, pack, fields), out_shape...  14.2 us
    unnamed x6, local copies, waits for them, and re-layouts  2.03 us
    cos x1, other arithmetic, wave_tables(): jnp.cos(inner)  1.28 us
    concatenate x1, other arithmetic, wave_tables(): jnp.concatenate([jnp.cos(inner), jnp.sin(inner), jnp.broadcast_to(jnp.cos...  1.15 us

commit v1 on v0

v1 whole, which is shorter than its diff:
```python
import functools
import math

import jax
import jax.numpy as jnp
from jax import lax
from jax.experimental import pallas as pl
from jax.experimental.pallas import tpu as pltpu
from jax.sharding import PartitionSpec as P

BLK = 128
SPAN = 2 * BLK
STREAMS = 2


def iota(shape, axis):
    return lax.broadcasted_iota(jnp.int32, shape, axis)


def unit(condition):
    return jnp.where(condition, 1.0, 0.0).astype(jnp.float32)


class Plan:
    def __init__(self, waves, fields, lat_count, lev_count, half_lat):
        self.waves, self.fields = waves, fields
        self.half_lat = half_lat
        self.devices = lat_count * lev_count
        self.rows = half_lat // self.devices
        self.hf = 2 * fields
        self.lanes = waves * 4 * fields
        self.share = max(
            n for n in range(1, self.rows + 1) if self.rows % n == 0 and (n == 1 or 4 * n * waves <= BLK)
        )
        self.groups = self.rows // self.share
        self.block = self.share * waves
        self.depth = 4 * self.block
        self.images = self.share * self.hf
        self.scale = (2.0 * waves) ** (-0.5)

    def tiles(self, group):
        last = ((group + 1) * self.share - 1) * self.devices + self.devices - 1
        return -(-(last + 6) // SPAN)

    def inside(self, group, tile):
        first = group * self.share * self.devices
        return (tile + 1) * SPAN - 1 < 3 + first - first // 2

    def scratch(self):
        return [
            pltpu.VMEM((self.groups, 4 * self.images, self.depth), jnp.bfloat16),
            pltpu.VMEM((self.groups, 4, self.block, BLK), jnp.float32),
            pltpu.VMEM((self.groups * 2 * self.block, 4 * self.images), jnp.float32),
            pltpu.VMEM((self.rows, BLK), jnp.float32),
        ]


def waves_at(deal, index, waves):
    out = jnp.zeros_like(index)
    for wave in range(waves):
        out = jnp.where(index == wave, deal[wave], out)
    return out


def fill_tables(plan, device, lengths, deal, table, row_length):
    wave = waves_at(deal, iota((plan.block, BLK), 0) % plan.waves, plan.waves).astype(jnp.float32)
    product = wave * iota((plan.block, BLK), 1).astype(jnp.float32)
    member = iota((plan.block, 1), 0) // plan.waves

    def fill(group, carry):
        length = jnp.zeros((plan.block, 1), jnp.float32)
        for each in range(plan.share):
            own = lengths[(group * plan.share + each) * plan.devices + device].astype(jnp.float32)
            length = jnp.where(member == each, own, length)
            row_length[pl.ds(group * plan.share + each, 1), :] = jnp.full((1, BLK), own, jnp.float32)
        turned = product - jnp.floor(product / length) * length
        angle = turned * (2.0 * math.pi) / length
        cosine, sine = jnp.cos(angle), jnp.sin(angle)
        last_cos, last_sin = cosine[:, BLK - 1 : BLK], sine[:, BLK - 1 : BLK]
        next_cos, next_sin = cosine[:, 1:2], sine[:, 1:2]
        table[group, 0] = cosine
        table[group, 1] = -sine
        table[group, 2] = jnp.broadcast_to(last_cos * next_cos - last_sin * next_sin, product.shape)
        table[group, 3] = jnp.broadcast_to(-last_sin * next_cos - last_cos * next_sin, product.shape)
        return carry

    lax.fori_loop(0, plan.groups, fill, 0)


def lane_waves(plan, deal):
    return waves_at(deal, iota((1, plan.lanes), 1) // (4 * plan.fields), plan.waves)


def live_rows(plan, device, deal):
    half_lat = plan.half_lat
    cut = lane_waves(plan, deal) * (half_lat // BLK) // (2 * half_lat)
    row = iota((plan.rows, 1), 0) * plan.devices + device
    return unit(row // BLK >= cut)


def image_sign(image, sine, odd):
    sign = jnp.ones(jnp.broadcast_shapes(sine.shape, odd.shape), jnp.float32)
    if image % 2:
        sign = sign * (1.0 - 2.0 * unit(sine))
    if image // 2:
        sign = sign * (1.0 - 2.0 * unit(odd))
    return sign


def mix_fields(plan, values, mixing_ref):
    fields = plan.fields
    pick = unit(iota((BLK, fields), 0) % fields == iota((BLK, fields), 1)).astype(jnp.bfloat16)
    across = (((1,), (1,)), ((), ()))
    half = lax.dot_general(
        pick, mixing_ref[...], across, preferred_element_type=jnp.float32
    ).astype(jnp.bfloat16)
    mixer = lax.dot_general(half, pick, across, preferred_element_type=jnp.float32)
    same = iota((BLK, BLK), 0) // fields == iota((BLK, BLK), 1) // fields
    mixer = jnp.where(same, mixer, 0.0).astype(jnp.bfloat16)
    return jnp.concatenate(
        [
            jnp.dot(values[:, at : at + BLK], mixer, preferred_element_type=jnp.float32)
            for at in range(0, plan.lanes, BLK)
        ],
        axis=1,
    )


def place_coefficients(plan, values, deal, mixing_ref, left):
    waves, fields, hf, lanes = plan.waves, plan.fields, plan.hf, plan.lanes
    mixed = plan.scale * mix_fields(plan, values, mixing_ref)
    high = mixed.astype(jnp.bfloat16).astype(jnp.float32)
    lane = iota((hf, lanes), 1)
    keep = unit(lane // (2 * fields) % 2 * fields + lane % fields == iota((hf, lanes), 0))
    rows = values.shape[0]
    spread = jnp.concatenate(
        [
            (source[:, None, :] * keep[None, :, :]).reshape(rows * hf, lanes).astype(jnp.bfloat16)
            for source in (high, mixed - high)
        ],
        axis=1,
    )
    down, right = iota((2 * lanes, plan.depth), 0), iota((2 * lanes, plan.depth), 1)
    down_kind = down // lanes * 2 + down % lanes // fields % 2
    down_wave = down % lanes // (4 * fields)
    gather = unit((down_kind == right // plan.block) & (down_wave == right % waves)).astype(jnp.bfloat16)
    placed = jnp.dot(spread, gather, preferred_element_type=jnp.float32)
    right = iota((1, plan.depth), 1)
    mine = unit(iota((plan.images, 1), 0) // hf == right % plan.block // waves)
    odd = waves_at(deal, right % waves, waves) % 2 == 1
    sine = right // plan.block % 2 == 1
    signs = [mine * image_sign(image, sine, odd) for image in range(4)]
    for group in range(rows // plan.share):
        own = placed[group * plan.images : (group + 1) * plan.images]
        for image in range(4):
            left[group, image * plan.images : (image + 1) * plan.images, :] = (
                own * signs[image]
            ).astype(jnp.bfloat16)


def walk_circles(plan, groups, device, lengths, table, left, total):
    position = iota((1, SPAN), 1)
    member = iota((plan.block, 1), 0) // plan.waves
    across = (((1,), (1,)), ((), ()))

    def phases(group, tile, cos_now, sin_now):
        step_cos, step_sin = table[group, 2], table[group, 3]
        cosines, sines = [], []
        for _ in range(SPAN // BLK):
            cosines.append(cos_now)
            sines.append(sin_now)
            cos_now, sin_now = (
                cos_now * step_cos - sin_now * step_sin,
                sin_now * step_cos + cos_now * step_sin,
            )
        cosine, sine = jnp.concatenate(cosines, axis=1), jnp.concatenate(sines, axis=1)
        near, far = cosine.astype(jnp.bfloat16), sine.astype(jnp.bfloat16)
        weights = jnp.concatenate([near, far, near, far], axis=0)
        if tile > 0 and plan.inside(group, tile):
            return cos_now, sin_now, weights, weights[: 2 * plan.block]
        at = position + tile * SPAN
        quarter = jnp.zeros((plan.block, 1), jnp.int32)
        for each in range(plan.share):
            own = lengths[(group * plan.share + each) * plan.devices + device]
            quarter = jnp.where(member == each, lax.shift_right_logical(own, 2), quarter)
        share = jnp.where(at < quarter, 1.0, jnp.where(at == quarter, 0.5, 0.0)).astype(jnp.float32)
        if tile == 0:
            share = share * jnp.where(at == 0, 0.5, 1.0).astype(jnp.float32)
        shared = jnp.concatenate([cosine * share, sine * share], axis=0).astype(jnp.bfloat16)
        return cos_now, sin_now, weights, shared

    streams = [[] for _ in range(STREAMS)]
    for group in sorted(groups, key=lambda group: -plan.tiles(group)):
        min(streams, key=len).extend((group, tile) for tile in range(plan.tiles(group)))
    state, sums, waiting = {}, {}, []

    def finish():
        for group, shared, grid in waiting:
            extra = lax.dot_general(
                shared,
                jnp.tanh(grid).astype(jnp.bfloat16),
                across,
                preferred_element_type=jnp.float32,
            )
            sums[group] = sums[group] + extra if group in sums else extra
        waiting.clear()

    for step in range(max(len(stream) for stream in streams)):
        started = []
        for stream in streams:
            if step < len(stream):
                group, tile = stream[step]
                if group not in state:
                    state[group] = table[group, 0], table[group, 1]
                cos_now, sin_now, weights, shared = phases(group, tile, *state[group])
                state[group] = cos_now, sin_now
                grid = jnp.dot(left[group], weights, preferred_element_type=jnp.float32)
                started.append((group, shared, grid))
        finish()
        waiting.extend(started)
    finish()
    size = 2 * plan.block
    for group in groups:
        total[group * size : (group + 1) * size, :] = sums[group]


def fold_circles(plan, sums, deal):
    waves, fields, hf, lanes = plan.waves, plan.fields, plan.hf, plan.lanes
    size, wide = 2 * plan.block, 4 * plan.images
    down, right = iota((size, wide), 0), iota((size, wide), 1)
    odd = waves_at(deal, down % waves, waves) % 2 == 1
    sine = down // plan.block == 1
    sign = jnp.zeros((size, wide), jnp.float32)
    for image in range(4):
        sign = jnp.where(right // plan.images == image, image_sign(image, sine, odd), sign)
    sign = sign * unit(down % plan.block // waves == right % plan.images // hf)
    count = sums.shape[0] // size
    signed = (sums.reshape(count, size, wide) * sign[None]).reshape(count * size, wide)
    high = signed.astype(jnp.bfloat16)
    low = (signed - high.astype(jnp.float32)).astype(jnp.bfloat16)
    down, right = iota((2 * wide, lanes), 0), iota((2 * wide, lanes), 1)
    spread = unit(down % hf == right // (2 * fields) % 2 * fields + right % fields).astype(jnp.bfloat16)
    folded = jnp.dot(
        jnp.concatenate([high, low], axis=1), spread, preferred_element_type=jnp.float32
    )
    down, right = iota((size, lanes), 0), iota((size, lanes), 1)
    keep = unit((down // plan.block == right // fields % 2) & (down % waves == right // (4 * fields)))
    kept = (folded.reshape(count, size, lanes) * keep[None]).reshape(count, 2, plan.share, waves, lanes)
    return jnp.sum(jnp.sum(kept, axis=1), axis=2).reshape(count * plan.share, lanes)


def circle_products(plan, values, length, deal):
    waves, lanes = plan.waves, plan.lanes
    wave = lane_waves(plan, deal).astype(jnp.float32)
    part = 1.0 - 2.0 * unit(iota((1, lanes), 1) // plan.fields % 2 == 1)
    inverse = 1.0 / length

    def whole(turns):
        return unit(turns == length * jnp.floor(turns * inverse + 0.5))

    out = jnp.zeros_like(values)
    for other in range(waves):
        at = other * 4 * plan.fields

        def turn(source):
            return jnp.concatenate([source[:, at:], source[:, :at]], axis=1) if at else source

        partner = turn(wave)
        gram = whole(wave - partner) + part * whole(wave + partner)
        out = out + gram * turn(values)
    return out * (0.5 * plan.scale) * length


def row_kernel(lengths, deal, fourier_ref, mixing_ref, out_ref, left, table, total, row_length):
    lat_count, count, block_width = fourier_ref.shape
    fields = mixing_ref.shape[0]
    plan = Plan(deal.shape[0], fields, lat_count, lax.axis_size("lev"), lengths.shape[0])
    rows = plan.rows
    pack = rows // count
    part_span = block_width // pack
    device = lax.axis_index("lev") * lat_count + lax.axis_index("lat")
    fill_tables(plan, device, lengths, deal, table, row_length)
    blocks = [fourier_ref[side].astype(jnp.float32) for side in range(lat_count)]
    values = jnp.concatenate(
        [
            jnp.concatenate(
                [block[:, part * part_span : (part + 1) * part_span] for block in blocks], axis=1
            )
            for part in range(pack)
        ],
        axis=0,
    )
    live = live_rows(plan, device, deal)
    values = values * live
    place_coefficients(plan, values.astype(jnp.bfloat16), deal, mixing_ref, left)
    walk_circles(plan, range(plan.groups), device, lengths, table, left, total)
    summed = fold_circles(plan, total[...], deal)
    length = jnp.concatenate([row_length[...]] * (plan.lanes // BLK), axis=1)
    row = (iota((rows, 1), 0) * plan.devices + device).astype(jnp.float32)
    weight = jnp.sin(math.pi * (row + 0.5) / (2 * plan.half_lat)) / jnp.sqrt(length)
    summed = (summed + circle_products(plan, values, length, deal)) * (weight * live)
    for side in range(lat_count):
        out_ref[side] = jnp.concatenate(
            [
                summed[
                    part * count : (part + 1) * count, side * part_span : (side + 1) * part_span
                ]
                for part in range(pack)
            ],
            axis=1,
        ).astype(jnp.bfloat16)


def rows_step(fourier, lengths, deal_list, mixing):
    lat_count, lev_count = lax.axis_size("lat"), lax.axis_size("lev")
    plan = Plan(deal_list.shape[0], mixing.shape[0], lat_count, lev_count, lengths.shape[0])
    vmem = pl.BlockSpec(memory_space=pltpu.VMEM)
    smem = pl.BlockSpec(memory_space=pltpu.SMEM)
    return pl.pallas_call(
        row_kernel,
        out_shape=jax.ShapeDtypeStruct(fourier.shape, jnp.bfloat16),
        in_specs=[smem, smem, vmem, vmem],
        out_specs=vmem,
        scratch_shapes=plan.scratch(),
    )(lengths, deal_list, fourier, mixing)


def column_masks(pattern_ref, local_cols):
    slots, blocks_down, blocks = pattern_ref.shape
    column = lax.broadcasted_iota(jnp.int32, (1, local_cols), 1)
    column = column + lax.axis_index("lev") * local_cols
    odd = (1 - 2 * (column % 2)).astype(jnp.float32)
    masks = []
    for slot in range(slots):
        mask = jnp.zeros((1, local_cols), jnp.float32)
        for block in range(blocks):
            kept = pattern_ref[slot, blocks_down - 1, block].astype(jnp.float32)
            mask = jnp.where(column // BLK == block, kept, mask)
        masks.append(mask)
    return odd, masks


def peers_of(axis):
    count = lax.axis_size(axis)
    return [lax.rem(lax.axis_index(axis) + off, count) for off in range(1, count)]


def greet():
    expect(hail())


def expect(total):
    pl.semaphore_wait(pltpu.get_barrier_semaphore(), total)


def hail():
    barrier = pltpu.get_barrier_semaphore()
    total = 0
    for axis in ("lat", "lev"):
        for peer in peers_of(axis):
            pl.semaphore_signal(
                barrier, inc=1, device_id={axis: peer}, device_id_type=pl.DeviceIdType.MESH
            )
            total += 1
    return total


def send(axis, sources, target, sems):
    copies = []
    for step, peer in enumerate(peers_of(axis)):
        copy = pltpu.make_async_remote_copy(
            src_ref=sources(peer),
            dst_ref=target,
            send_sem=sems.at[0, step],
            recv_sem=sems.at[1, step],
            device_id={axis: peer},
            device_id_type=pl.DeviceIdType.MESH,
        )
        copy.start()
        copies.append(copy)
    return copies


def inward_kernel(pack, pattern_ref, spec_ref, legendre_ref, out_ref, turned, leaving, arriving, summed, landed,
                  lev_sems, lat_sems):
    slots, _, half_lat = legendre_ref.shape
    lev_count, lat_count, count, width = leaving.shape
    devices = lev_count * lat_count
    lev_index, lat_index = lax.axis_index("lev"), lax.axis_index("lat")
    packed = half_lat // pack
    greetings = hail()
    odd, masks = column_masks(pattern_ref, legendre_ref.shape[1])
    sums = []
    for slot in range(slots):
        kept = jnp.concatenate([spec_ref[slot, 0], spec_ref[slot, 1]], axis=0).astype(jnp.float32)
        kept = kept * masks[slot]
        sums.append(
            jnp.dot(
                jnp.concatenate([kept, kept * odd], axis=0).astype(jnp.bfloat16),
                legendre_ref[slot],
                preferred_element_type=jnp.float32,
            )
        )
    for block in range(packed // BLK):
        piece = jnp.concatenate(
            [
                value[:, part * packed + block * BLK : part * packed + (block + 1) * BLK]
                for part in range(pack)
                for value in sums
            ],
            axis=0,
        )
        turned[:, block * BLK : (block + 1) * BLK, :] = jnp.stack(
            [piece[at : at + BLK].T for at in range(0, width, BLK)]
        )
    for device in range(devices):
        for at in range(width // BLK):
            leaving[device // lat_count, device % lat_count, :, at * BLK : (at + 1) * BLK] = (
                turned[at, pl.ds(device, count, stride=devices), :].astype(jnp.bfloat16)
            )
    expect(greetings)
    copies = send("lev", lambda peer: leaving.at[peer], arriving.at[lev_index], lev_sems)
    mine = lev_index * lat_count
    total = jnp.stack(
        [
            jnp.concatenate(
                [
                    turned[at, pl.ds(mine + side, count, stride=devices), :]
                    for at in range(width // BLK)
                ],
                axis=1,
            )
            for side in range(lat_count)
        ]
    )
    for copy, peer in zip(copies, [lax.rem(lev_index + lev_count - off, lev_count) for off in range(1, lev_count)]):
        copy.wait_recv()
        total = total + arriving[peer].astype(jnp.float32)
    summed[...] = total.astype(jnp.bfloat16)
    crossing = send("lat", lambda peer: summed.at[peer], landed.at[lat_index], lat_sems)
    out_ref[lat_index] = summed[lat_index]
    for copy, peer in zip(crossing, [lax.rem(lat_index + lat_count - off, lat_count) for off in range(1, lat_count)]):
        copy.wait_recv()
        out_ref[peer] = landed[peer]
    for copy in copies + crossing:
        copy.wait_send()


def outward_kernel(pack, fields, pattern_ref, rows_ref, legendre_ref, out_ref, held, landed, gathered, turned,
                   lev_sems, lat_sems, load_sem):
    slots, local_cols, half_lat = held.shape
    lev_count, lat_count, count, width = gathered.shape
    devices = lev_count * lat_count
    lev_index, lat_index = lax.axis_index("lev"), lax.axis_index("lat")
    packed = half_lat // pack
    part_width = 4 * fields
    load = pltpu.make_async_copy(legendre_ref, held, load_sem)
    load.start()
    greet()
    crossing = send("lat", lambda peer: rows_ref.at[peer], landed.at[lat_index], lat_sems)
    landed[lat_index] = rows_ref[lat_index]
    for copy in crossing:
        copy.wait_recv()
    copies = send("lev", lambda peer: landed, gathered.at[lev_index], lev_sems)
    gathered[lev_index] = landed[...]
    for copy in copies:
        copy.wait_recv()
    for device in range(devices):
        block = gathered[device // lat_count, device % lat_count].astype(jnp.float32)
        for at in range(width // BLK):
            turned[at, pl.ds(device, count, stride=devices), :] = block[:, at * BLK : (at + 1) * BLK]
    load.wait()
    odd, masks = column_masks(pattern_ref, local_cols)
    sides = [turned[at].astype(jnp.bfloat16) for at in range(width // BLK)]
    for slot in range(slots):
        total = None
        for part in range(pack):
            at = part * slots * part_width + slot * part_width
            value = jnp.dot(
                held[slot, :, part * packed : (part + 1) * packed],
                sides[at // BLK],
                preferred_element_type=jnp.float32,
            )[:, at % BLK : at % BLK + part_width]
            total = value if total is None else total + value
        flat = total.T
        joined = flat[: 2 * fields] + odd * flat[2 * fields :]
        out_ref[slot] = joined * masks[slot]
    for copy in copies + crossing:
        copy.wait_send()


def local(spec_in, legendre, pattern, deal_list, circle_lengths, mixing):
    lat_index = lax.axis_index("lat")
    lev_index = lax.axis_index("lev")
    lat_count = lax.axis_size("lat")
    lev_count = lax.axis_size("lev")
    slots, local_cols, half_lat = legendre.shape
    fields = spec_in.shape[2]
    devices = lat_count * lev_count
    rows = half_lat // devices
    span = 4 * slots * fields
    pack = max(1, BLK // span)
    count, width = rows // pack, span * pack
    vmem = pl.BlockSpec(memory_space=pltpu.VMEM)
    block_shape = (lat_count, count, width)
    sems = [
        pltpu.SemaphoreType.DMA((2, lev_count)),
        pltpu.SemaphoreType.DMA((2, lat_count)),
    ]
    turned = pltpu.VMEM((width // BLK, half_lat // pack, BLK), jnp.float32)
    fourier = pl.pallas_call(
        functools.partial(inward_kernel, pack),
        out_shape=jax.ShapeDtypeStruct(block_shape, jnp.bfloat16),
        in_specs=[pl.BlockSpec(memory_space=pltpu.SMEM), vmem, vmem],
        out_specs=vmem,
        scratch_shapes=[
            turned,
            pltpu.VMEM((lev_count,) + block_shape, jnp.bfloat16),
            pltpu.VMEM((lev_count,) + block_shape, jnp.bfloat16),
            pltpu.VMEM(block_shape, jnp.bfloat16),
            pltpu.VMEM(block_shape, jnp.bfloat16),
        ]
        + sems,
        compiler_params=pltpu.CompilerParams(collective_id=0, has_side_effects=True),
    )(pattern, spec_in, legendre)
    leaving = rows_step(fourier, circle_lengths, deal_list, mixing)
    product = pl.pallas_call(
        functools.partial(outward_kernel, pack, fields),
        out_shape=jax.ShapeDtypeStruct((slots, 2 * fields, local_cols), jnp.float32),
        in_specs=[
            pl.BlockSpec(memory_space=pltpu.SMEM),
            vmem,
            pl.BlockSpec(memory_space=pl.ANY),
        ],
        out_specs=vmem,
        scratch_shapes=[
            pltpu.VMEM(legendre.shape, jnp.bfloat16),
            pltpu.VMEM(block_shape, jnp.bfloat16),
            pltpu.VMEM((lev_count,) + block_shape, jnp.bfloat16),
            turned,
        ]
        + sems
        + [pltpu.SemaphoreType.DMA],
        compiler_params=pltpu.CompilerParams(collective_id=1, has_side_effects=True),
    )(pattern, leaving, legendre)
    return product.reshape(slots, 2, fields, local_cols)


def solution(mesh):
    return jax.shard_map(
        local,
        mesh=mesh,
        in_specs=(
            P("lat", None, None, "lev"),
            P("lat", "lev", None),
            P("lat", None, None),
            P(),
            P(),
            P(),
        ),
        out_specs=P("lat", None, None, "lev"),
        check_vma=False,
    )
```

time: 57.5 us -> 49.9 us (0.87)
  other arithmetic: 4.18 us -> 0 us
  Pallas kernels: 48.8 us -> 46.7 us
  local copies, waits for them, and re-layouts: 4.09 us -> 2.76 us
    pallas_call x1, Pallas kernels: 18 us -> 16.5 us  [rows_step(): pl.pallas_call(row_kernel, out_shape=jax.ShapeDtypeStruct(fourier.shape,...]
    cos x2 -> x0, other arithmetic: 1.39 us -> none  [the longest x1 1.28 us: wave_tables(): jnp.cos(inner)]
    concatenate x1 -> x0, other arithmetic: 1.15 us -> none  [wave_tables(): jnp.concatenate([jnp.cos(inner), jnp.sin(inner), jnp.broadcast_to(jnp.cos...]
    reshape x1 -> x0, local copies, waits for them, and re-layouts: 0.78 us -> none  [local(): by_device = circle_lengths.reshape(rows, devices)]
    mul x4 -> x0, other arithmetic: 0.74 us -> none  [the longest x2 0.73 us: angle_of(): product = wave * position]
    div x1 -> x0, local copies, waits for them, and re-layouts: 0.73 us -> none  [rows_step(): jnp.sin(math.pi * (row_ids.astype(jnp.float32) + 0.5) / (2 * half_lat))]
    unnamed x6 -> x2, local copies, waits for them, and re-layouts: 2.03 us -> 2.76 us
    convert_element_type x2 -> x0, other arithmetic: 0.66 us -> none  [the longest x1 0.66 us: wave_tables(): wave = deal_list.astype(jnp.float32)[None, :, None]]
where the time goes in v1:
time: 49.9 us; the launch traced here: 49.5 us
  Pallas kernels  46.7 us (94%)
  local copies, waits for them, and re-layouts  2.76 us (6%)
    pallas_call x1, Pallas kernels, local(): pl.pallas_call(functools.partial(inward_kernel, pack), out_shape=jax.Shap...  16.7 us
    pallas_call x1, Pallas kernels, rows_step(): pl.pallas_call(row_kernel, out_shape=jax.ShapeDtypeStruct(fourier.shape,...  16.5 us
    pallas_call x1, Pallas kernels, local(): pl.pallas_call(functools.partial(outward_kernel, pack, fields), out_shape...  13.6 us
    unnamed x2, local copies, waits for them, and re-layouts  2.76 us

profile of v1, /device:TPU:0, one launch (start us, length us, event | category | flops | bytes accessed | tf_op | source)
XLA Modules:
  0.0 49.5 jit_solution(3849233280394696252)
XLA Ops:
  0.0 1.3 %copy.8.pattern_ref = s32[2,20,20]{2,1,0:T(8,128)} copy(s32[2,20,20]{2,0,1:T(2,128)} %param.8) | data formatting | bytes 6400 | tf_op args[2]
  1.3 16.7 %shard_map.64.fourier_ref = bf16[4,40,128]{2,1,0:T(8,128)(2,1)} custom-call(s32[2,20,20]{2,1,0:T(8,128)} %copy.8.pattern_ref, bf16[2,2,8,320]{3,2,1,0:T(8,128)(2,1)} %spec_ref.1, bf16[2,320,2560]{2,1,0:T(8,128)(2,1)} %legendre_ref.3), custom_call_target="tpu_custom_call" | custom-call | tf_op jit(solution)/shard_map/pallas_call | solution.py:511
  18.0 16.5 %shard_map.65.rows_ref = bf16[4,40,128]{2,1,0:T(8,128)(2,1)} custom-call(s32[2560]{0:T(1024)} %lengths.1, s32[8]{0:T(128)} %deal.1, bf16[4,40,128]{2,1,0:T(8,128)(2,1)} %shard_map.64.fourier_ref, bf16[8,8]{1,0:T(8,128)(2,1)} %mixing_ref.1), custom_call_target="tpu_custom_call" | custom-call | tf_op jit(solution)/shard_map/pallas_call | solution.py:319
  34.5 13.6 %shard_map.66 = f32[2,16,320]{2,1,0:T(8,128)} custom-call(s32[2,20,20]{2,1,0:T(8,128)} %copy.8.pattern_ref, bf16[4,40,128]{2,1,0:T(8,128)(2,1)} %shard_map.65.rows_ref, bf16[2,320,2560]{2,1,0:T(8,128)(2,1)} %legendre_ref.3), custom_call_target="tpu_custom_call" | custom-call | tf_op jit(solution)/shard_map/pallas_call | solution.py:527
  48.1 1.4 %copy.10 = f32[2,2,8,320]{3,2,1,0:T(8,128)} copy(f32[2,2,8,320]{3,2,1,0:T(8,128)} %bitcast.1) | data formatting | bytes 81920

commit v2 on v1

v2 whole, which is shorter than its diff:
```python
import functools
import math

import jax
import jax.numpy as jnp
from jax import lax
from jax.experimental import pallas as pl
from jax.experimental.pallas import tpu as pltpu
from jax.sharding import PartitionSpec as P

BLK = 128
SPAN = 2 * BLK
ACROSS = (((1,), (1,)), ((), ()))
STREAMS = 2
SPLIT = (3, 3)


def iota(shape, axis):
    return lax.broadcasted_iota(jnp.int32, shape, axis)


def unit(condition):
    return jnp.where(condition, 1.0, 0.0).astype(jnp.float32)


class Plan:
    def __init__(self, waves, fields, lat_count, lev_count, half_lat):
        self.waves, self.fields = waves, fields
        self.half_lat = half_lat
        self.devices = lat_count * lev_count
        self.rows = half_lat // self.devices
        self.hf = 2 * fields
        self.lanes = waves * 4 * fields
        self.share = max(
            n for n in range(1, self.rows + 1) if self.rows % n == 0 and (n == 1 or 4 * n * waves <= BLK)
        )
        self.groups = self.rows // self.share
        self.block = self.share * waves
        self.depth = 4 * self.block
        self.images = self.share * self.hf
        self.scale = (2.0 * waves) ** (-0.5)

    def tiles(self, group):
        last = ((group + 1) * self.share - 1) * self.devices + self.devices - 1
        return -(-(last + 6) // SPAN)

    def inside(self, group, tile):
        first = group * self.share * self.devices
        return (tile + 1) * SPAN - 1 < 3 + first - first // 2

    def chunks(self, pack):
        least = pack
        while least * self.devices % (pack * BLK) or least % self.share:
            least += pack
        units, out = self.rows // least, []
        first = self.rows
        for tenths in SPLIT:
            count = units * tenths // 10 * least
            if 0 < count < first:
                first -= count
                out.append((first, count))
        return out + [(0, first)]


def waves_at(deal, index, waves):
    out = jnp.zeros_like(index)
    for wave in range(waves):
        out = jnp.where(index == wave, deal[wave], out)
    return out


def fill_tables(plan, device, lengths, deal, table, row_length):
    wave = waves_at(deal, iota((plan.block, BLK), 0) % plan.waves, plan.waves).astype(jnp.float32)
    product = wave * iota((plan.block, BLK), 1).astype(jnp.float32)
    member = iota((plan.block, 1), 0) // plan.waves

    def fill(group, carry):
        length = jnp.zeros((plan.block, 1), jnp.float32)
        for each in range(plan.share):
            own = lengths[(group * plan.share + each) * plan.devices + device].astype(jnp.float32)
            length = jnp.where(member == each, own, length)
            row_length[pl.ds(group * plan.share + each, 1), :] = jnp.full((1, BLK), own, jnp.float32)
        turned = product - jnp.floor(product / length) * length
        angle = turned * (2.0 * math.pi) / length
        cosine, sine = jnp.cos(angle), jnp.sin(angle)
        last_cos, last_sin = cosine[:, BLK - 1 : BLK], sine[:, BLK - 1 : BLK]
        next_cos, next_sin = cosine[:, 1:2], sine[:, 1:2]
        table[group, 0] = cosine
        table[group, 1] = -sine
        table[group, 2] = jnp.broadcast_to(last_cos * next_cos - last_sin * next_sin, product.shape)
        table[group, 3] = jnp.broadcast_to(-last_sin * next_cos - last_cos * next_sin, product.shape)
        return carry

    lax.fori_loop(0, plan.groups, fill, 0)


def lane_waves(plan, deal):
    return waves_at(deal, iota((1, plan.lanes), 1) // (4 * plan.fields), plan.waves)


def live_rows(plan, device, deal):
    half_lat = plan.half_lat
    cut = lane_waves(plan, deal) * (half_lat // BLK) // (2 * half_lat)
    row = iota((plan.rows, 1), 0) * plan.devices + device
    return unit(row // BLK >= cut)


def image_sign(image, sine, odd):
    sign = jnp.ones(jnp.broadcast_shapes(sine.shape, odd.shape), jnp.float32)
    if image % 2:
        sign = sign * (1.0 - 2.0 * unit(sine))
    if image // 2:
        sign = sign * (1.0 - 2.0 * unit(odd))
    return sign


def fill_constants(plan, deal, mixing_ref, keep, gather, placed_sign, mixer, sum_sign, spread, fold_keep):
    waves, fields, hf, lanes = plan.waves, plan.fields, plan.hf, plan.lanes
    lane = iota((hf, lanes), 1)
    keep[...] = unit(lane // (2 * fields) % 2 * fields + lane % fields == iota((hf, lanes), 0))
    down, right = iota((2 * lanes, plan.depth), 0), iota((2 * lanes, plan.depth), 1)
    down_kind = down // lanes * 2 + down % lanes // fields % 2
    down_wave = down % lanes // (4 * fields)
    gather[...] = unit(
        (down_kind == right // plan.block) & (down_wave == right % waves)
    ).astype(jnp.bfloat16)
    right = iota((1, plan.depth), 1)
    mine = unit(iota((plan.images, 1), 0) // hf == right % plan.block // waves)
    odd = waves_at(deal, right % waves, waves) % 2 == 1
    sine = right // plan.block % 2 == 1
    for image in range(4):
        placed_sign[image] = mine * image_sign(image, sine, odd)
    pick = unit(iota((BLK, fields), 0) % fields == iota((BLK, fields), 1)).astype(jnp.bfloat16)
    half = lax.dot_general(
        pick, mixing_ref[...], ACROSS, preferred_element_type=jnp.float32
    ).astype(jnp.bfloat16)
    whole = lax.dot_general(half, pick, ACROSS, preferred_element_type=jnp.float32)
    same = iota((BLK, BLK), 0) // fields == iota((BLK, BLK), 1) // fields
    mixer[...] = jnp.where(same, whole, 0.0).astype(jnp.bfloat16)
    size, wide = sum_sign.shape
    down, right = iota((size, wide), 0), iota((size, wide), 1)
    odd = waves_at(deal, down % waves, waves) % 2 == 1
    sine = down // plan.block == 1
    sign = jnp.zeros((size, wide), jnp.float32)
    for image in range(4):
        sign = jnp.where(right // plan.images == image, image_sign(image, sine, odd), sign)
    sum_sign[...] = sign * unit(down % plan.block // waves == right % plan.images // hf)
    down, right = iota((2 * wide, lanes), 0), iota((2 * wide, lanes), 1)
    spread[...] = unit(
        down % hf == right // (2 * fields) % 2 * fields + right % fields
    ).astype(jnp.bfloat16)
    down, right = iota((size, lanes), 0), iota((size, lanes), 1)
    fold_keep[...] = unit(
        (down // plan.block == right // fields % 2) & (down % waves == right // (4 * fields))
    )


def fill_products(plan, device, row_length, deal, products, weights):
    length = jnp.concatenate([row_length[...]] * (plan.lanes // BLK), axis=1)
    wave = lane_waves(plan, deal).astype(jnp.float32)
    part = 1.0 - 2.0 * unit(iota((1, plan.lanes), 1) // plan.fields % 2 == 1)
    inverse, half = 1.0 / length, (0.5 * plan.scale) * length

    def whole(turns):
        return unit(turns == length * jnp.floor(turns * inverse + 0.5))

    for other in range(plan.waves):
        partner = rolled(plan, wave, other)
        products[other] = half * (whole(wave - partner) + part * whole(wave + partner))
    row = (iota((plan.rows, 1), 0) * plan.devices + device).astype(jnp.float32)
    weight = jnp.sin(math.pi * (row + 0.5) / (2 * plan.half_lat)) / jnp.sqrt(row_length[...])
    weights[0] = live_rows(plan, device, deal)
    weights[1] = weights[0] * jnp.concatenate([weight] * (plan.lanes // BLK), axis=1)


def rolled(plan, source, other):
    at = other * 4 * plan.fields
    return jnp.concatenate([source[:, at:], source[:, :at]], axis=1) if at else source


def place_coefficients(plan, first, values, keep, gather, placed_sign, mixer, left):
    rows = values.shape[0]
    narrow = values.astype(jnp.bfloat16)
    mixed = plan.scale * jnp.concatenate(
        [
            jnp.dot(narrow[:, at : at + BLK], mixer[...], preferred_element_type=jnp.float32)
            for at in range(0, plan.lanes, BLK)
        ],
        axis=1,
    )
    high = mixed.astype(jnp.bfloat16).astype(jnp.float32)
    spread = jnp.concatenate(
        [
            (source[:, None, :] * keep[...][None]).reshape(rows * plan.hf, plan.lanes).astype(jnp.bfloat16)
            for source in (high, mixed - high)
        ],
        axis=1,
    )
    placed = jnp.dot(spread, gather[...], preferred_element_type=jnp.float32)
    for group in range(rows // plan.share):
        own = placed[group * plan.images : (group + 1) * plan.images]
        for image in range(4):
            left[
                first // plan.share + group, image * plan.images : (image + 1) * plan.images, :
            ] = (own * placed_sign[image]).astype(jnp.bfloat16)


def walk_circles(plan, groups, device, lengths, table, left, total):
    position = iota((1, SPAN), 1)
    member = iota((plan.block, 1), 0) // plan.waves

    def phases(group, tile, cos_now, sin_now):
        step_cos, step_sin = table[group, 2], table[group, 3]
        cosines, sines = [], []
        for _ in range(SPAN // BLK):
            cosines.append(cos_now)
            sines.append(sin_now)
            cos_now, sin_now = (
                cos_now * step_cos - sin_now * step_sin,
                sin_now * step_cos + cos_now * step_sin,
            )
        cosine, sine = jnp.concatenate(cosines, axis=1), jnp.concatenate(sines, axis=1)
        near, far = cosine.astype(jnp.bfloat16), sine.astype(jnp.bfloat16)
        weights = jnp.concatenate([near, far, near, far], axis=0)
        if tile > 0 and plan.inside(group, tile):
            return cos_now, sin_now, weights, weights[: 2 * plan.block]
        at = position + tile * SPAN
        quarter = jnp.zeros((plan.block, 1), jnp.int32)
        for each in range(plan.share):
            own = lengths[(group * plan.share + each) * plan.devices + device]
            quarter = jnp.where(member == each, lax.shift_right_logical(own, 2), quarter)
        share = jnp.where(at < quarter, 1.0, jnp.where(at == quarter, 0.5, 0.0)).astype(jnp.float32)
        if tile == 0:
            share = share * jnp.where(at == 0, 0.5, 1.0).astype(jnp.float32)
        shared = jnp.concatenate([cosine * share, sine * share], axis=0).astype(jnp.bfloat16)
        return cos_now, sin_now, weights, shared

    streams = [[] for _ in range(STREAMS)]
    for group in sorted(groups, key=lambda group: -plan.tiles(group)):
        min(streams, key=len).extend((group, tile) for tile in range(plan.tiles(group)))
    state, sums, waiting = {}, {}, []

    def finish():
        for group, shared, grid in waiting:
            extra = lax.dot_general(
                shared,
                jnp.tanh(grid).astype(jnp.bfloat16),
                ACROSS,
                preferred_element_type=jnp.float32,
            )
            sums[group] = sums[group] + extra if group in sums else extra
        waiting.clear()

    for step in range(max(len(stream) for stream in streams)):
        started = []
        for stream in streams:
            if step < len(stream):
                group, tile = stream[step]
                if group not in state:
                    state[group] = table[group, 0], table[group, 1]
                cos_now, sin_now, weights, shared = phases(group, tile, *state[group])
                state[group] = cos_now, sin_now
                grid = jnp.dot(left[group], weights, preferred_element_type=jnp.float32)
                started.append((group, shared, grid))
        finish()
        waiting.extend(started)
    finish()
    size = 2 * plan.block
    for group in groups:
        total[group * size : (group + 1) * size, :] = sums[group]


def fold_circles(plan, sums, sum_sign, spread, fold_keep):
    size, wide = sum_sign.shape
    count = sums.shape[0] // size
    signed = (sums.reshape(count, size, wide) * sum_sign[...][None]).reshape(count * size, wide)
    high = signed.astype(jnp.bfloat16)
    low = (signed - high.astype(jnp.float32)).astype(jnp.bfloat16)
    folded = jnp.dot(
        jnp.concatenate([high, low], axis=1), spread[...], preferred_element_type=jnp.float32
    )
    kept = (folded.reshape(count, size, plan.lanes) * fold_keep[...][None]).reshape(
        count, 2, plan.share, plan.waves, plan.lanes
    )
    return jnp.sum(jnp.sum(kept, axis=1), axis=2).reshape(count * plan.share, plan.lanes)


def column_masks(plan, deal, slots, local_cols):
    column = iota((1, local_cols), 1) + lax.axis_index("lev") * local_cols
    odd = (1 - 2 * (column % 2)).astype(jnp.float32)
    masks = []
    for slot in range(slots):
        wave = deal[lax.axis_index("lat") * slots + slot]
        masks.append(unit(column // BLK * BLK <= plan.half_lat - 1 - wave))
    return odd, masks


def peers_of(axis):
    count = lax.axis_size(axis)
    return [lax.rem(lax.axis_index(axis) + off, count) for off in range(1, count)]


def expect(total):
    pl.semaphore_wait(pltpu.get_barrier_semaphore(), total)


def hail():
    barrier = pltpu.get_barrier_semaphore()
    total = 0
    for axis in ("lat", "lev"):
        for peer in peers_of(axis):
            pl.semaphore_signal(
                barrier, inc=1, device_id={axis: peer}, device_id_type=pl.DeviceIdType.MESH
            )
            total += 1
    return total


def send(axis, sources, target, sems):
    copies = []
    for step, peer in enumerate(peers_of(axis)):
        copy = pltpu.make_async_remote_copy(
            src_ref=sources(peer),
            dst_ref=target,
            send_sem=sems.at[0, step],
            recv_sem=sems.at[1, step],
            device_id={axis: peer},
            device_id_type=pl.DeviceIdType.MESH,
        )
        copy.start()
        copies.append(copy)
    return copies


def arrivals(axis, copies):
    count, index = lax.axis_size(axis), lax.axis_index(axis)
    for off, copy in enumerate(copies, 1):
        copy.wait_recv()
        yield lax.rem(index + count - off, count)


def chunk_scratch(count, pack, width, lat_count, lev_count):
    block = (lat_count, count // pack, width)
    devices = lat_count * lev_count
    return [
        pltpu.VMEM((lev_count,) + block, jnp.bfloat16),
        pltpu.VMEM((lev_count,) + block, jnp.bfloat16),
        pltpu.VMEM(block, jnp.bfloat16),
        pltpu.VMEM(block, jnp.bfloat16),
        pltpu.VMEM(block, jnp.bfloat16),
        pltpu.VMEM(block, jnp.bfloat16),
        pltpu.VMEM((lev_count,) + block, jnp.bfloat16),
        pltpu.VMEM((width // BLK, count // pack * devices, BLK), jnp.float32),
        pltpu.SemaphoreType.DMA((2, 2, lev_count)),
        pltpu.SemaphoreType.DMA((2, 2, lat_count)),
    ]


CHUNK_REFS = 10


def round_trip_kernel(plan, pack, chunks, lengths, deal, spec_ref, legendre_ref, mixing_ref, out_ref, *scratch):
    held, load_sems, left, table, total, row_length, products, weights, values_ref = scratch[:9]
    keep, gather, placed_sign, mixer, sum_sign, spread, fold_keep = scratch[9:16]
    buffers = [
        scratch[16 + at * CHUNK_REFS : 16 + (at + 1) * CHUNK_REFS] for at in range(len(chunks))
    ]
    slots, local_cols, half_lat = held.shape
    fields, devices = plan.fields, plan.devices
    lat_count, lev_count = lax.axis_size("lat"), lax.axis_size("lev")
    lev_index, lat_index = lax.axis_index("lev"), lax.axis_index("lat")
    device = lev_index * lat_count + lat_index
    part_width = 4 * fields
    part_span = slots * part_width
    width = part_span * pack
    faces = width // BLK
    loads = []
    for at, (first, count) in enumerate(chunks):
        columns = pl.ds(first * devices, count * devices)
        load = pltpu.make_async_copy(
            legendre_ref.at[:, :, columns], held.at[:, :, columns], load_sems.at[at]
        )
        load.start()
        loads.append(load)
    greetings = hail()
    odd, masks = column_masks(plan, deal, slots, local_cols)
    lefts = []
    for slot in range(slots):
        kept = jnp.concatenate([spec_ref[slot, 0], spec_ref[slot, 1]], axis=0).astype(jnp.float32)
        kept = kept * masks[slot]
        lefts.append(jnp.concatenate([kept, kept * odd], axis=0).astype(jnp.bfloat16))

    sent = []
    for at, (first, count) in enumerate(chunks):
        leaving, arriving, turned, lev_sems = (buffers[at][n] for n in (0, 1, 7, 8))
        each = count // pack
        loads[at].wait()
        sums = [
            jnp.dot(
                lefts[slot],
                held[slot, :, first * devices : (first + count) * devices],
                preferred_element_type=jnp.float32,
            )
            for slot in range(slots)
        ]
        for block in range(each * devices // BLK):
            piece = jnp.concatenate(
                [
                    value[:, part * each * devices + block * BLK : part * each * devices + (block + 1) * BLK]
                    for part in range(pack)
                    for value in sums
                ],
                axis=0,
            )
            for face in range(faces):
                turned[face, block * BLK : (block + 1) * BLK, :] = piece[face * BLK : (face + 1) * BLK].T
        for target in range(devices):
            for face in range(faces):
                leaving[target // lat_count, target % lat_count, :, face * BLK : (face + 1) * BLK] = (
                    turned[face, pl.ds(target, each, stride=devices), :].astype(jnp.bfloat16)
                )
        if at == 0:
            expect(greetings)
        sent.append(send("lev", lambda peer, leaving=leaving: leaving.at[peer], arriving.at[lev_index], lev_sems.at[0]))
    finished = list(sent)

    fill_constants(plan, deal, mixing_ref, keep, gather, placed_sign, mixer, sum_sign, spread, fold_keep)
    fill_tables(plan, device, lengths, deal, table, row_length)

    crossed = []
    for at, (first, count) in enumerate(chunks):
        arriving, summed, landed, turned, lat_sems = (buffers[at][n] for n in (1, 2, 3, 7, 9))
        each = count // pack
        sum_of = jnp.stack(
            [
                jnp.concatenate(
                    [
                        turned[face, pl.ds(lev_index * lat_count + side, each, stride=devices), :]
                        for face in range(faces)
                    ],
                    axis=1,
                )
                for side in range(lat_count)
            ]
        )
        for peer in arrivals("lev", sent[at]):
            sum_of = sum_of + arriving[peer].astype(jnp.float32)
        summed[...] = sum_of.astype(jnp.bfloat16)
        crossed.append(
            send("lat", lambda peer, summed=summed: summed.at[peer], landed.at[lat_index], lat_sems.at[0])
        )
        landed[lat_index] = summed[lat_index]
        if at == 0:
            fill_products(plan, device, row_length, deal, products, weights)
    finished += crossed

    returned, shared = [], []

    def pass_on(at):
        back, gathered, lev_sems = (buffers[at][n] for n in (5, 6, 8))
        for _ in arrivals("lat", returned[at]):
            pass
        copies = send("lev", lambda peer: back, gathered.at[lev_index], lev_sems.at[1])
        gathered[lev_index] = back[...]
        shared.append(copies)
        finished.append(copies)

    for at, (first, count) in enumerate(chunks):
        landed, leaving_rows, back, lat_sems = (buffers[at][n] for n in (3, 4, 5, 9))
        each = count // pack
        for _ in arrivals("lat", crossed[at]):
            pass
        blocks = [landed[side].astype(jnp.float32) for side in range(lat_count)]
        values = jnp.concatenate(
            [
                jnp.concatenate(
                    [block[:, part * part_span : (part + 1) * part_span] for block in blocks], axis=1
                )
                for part in range(pack)
            ],
            axis=0,
        )
        values = values * weights[0, first : first + count]
        values_ref[first : first + count] = values
        place_coefficients(plan, first, values, keep, gather, placed_sign, mixer, left)
        groups = list(range(first // plan.share, (first + count) // plan.share))
        if at:
            middle = len(groups) // 2
            walk_circles(plan, groups[middle:], device, lengths, table, left, total)
            pass_on(at - 1)
            groups = groups[:middle]
        if groups:
            walk_circles(plan, groups, device, lengths, table, left, total)
        size = 2 * plan.block
        result = fold_circles(
            plan,
            total[first // plan.share * size : (first + count) // plan.share * size, :],
            sum_sign,
            spread,
            fold_keep,
        )
        values = values_ref[first : first + count]
        for other in range(plan.waves):
            result = result + products[other, first : first + count] * rolled(plan, values, other)
        result = result * weights[1, first : first + count]
        for side in range(lat_count):
            leaving_rows[side] = jnp.concatenate(
                [
                    result[part * each : (part + 1) * each, side * part_span : (side + 1) * part_span]
                    for part in range(pack)
                ],
                axis=1,
            ).astype(jnp.bfloat16)
        returned.append(
            send("lat", lambda peer, rows=leaving_rows: rows.at[peer], back.at[lat_index], lat_sems.at[1])
        )
        back[lat_index] = leaving_rows[lat_index]
    finished += returned

    sums = [None] * slots
    for at, (first, count) in enumerate(chunks):
        gathered, turned = buffers[at][6], buffers[at][7]
        each = count // pack
        if at == len(chunks) - 1:
            pass_on(at)
        for _ in arrivals("lev", shared[at]):
            pass
        for source in range(devices):
            block = gathered[source // lat_count, source % lat_count].astype(jnp.float32)
            for face in range(faces):
                turned[face, pl.ds(source, each, stride=devices), :] = block[:, face * BLK : (face + 1) * BLK]
        sides = [turned[face].astype(jnp.bfloat16) for face in range(faces)]
        for slot in range(slots):
            for part in range(pack):
                lane = part * part_span + slot * part_width
                start = (first + part * each) * devices
                value = jnp.dot(
                    held[slot, :, start : start + each * devices],
                    sides[lane // BLK],
                    preferred_element_type=jnp.float32,
                )[:, lane % BLK : lane % BLK + part_width]
                sums[slot] = value if sums[slot] is None else sums[slot] + value
    odd, masks = column_masks(plan, deal, slots, local_cols)
    for slot in range(slots):
        flat = sums[slot].T
        out_ref[slot] = (flat[: 2 * fields] + odd * flat[2 * fields :]) * masks[slot]
    for copies in finished:
        for copy in copies:
            copy.wait_send()


def local(spec_in, legendre, pattern, deal_list, circle_lengths, mixing):
    lat_count, lev_count = lax.axis_size("lat"), lax.axis_size("lev")
    slots, local_cols, half_lat = legendre.shape
    fields, waves = spec_in.shape[2], deal_list.shape[0]
    plan = Plan(waves, fields, lat_count, lev_count, half_lat)
    span = 4 * slots * fields
    pack = max(1, BLK // span)
    chunks = plan.chunks(pack)
    vmem = pl.BlockSpec(memory_space=pltpu.VMEM)
    smem = pl.BlockSpec(memory_space=pltpu.SMEM)
    size, wide = 2 * plan.block, 4 * plan.images
    scratch = [
        pltpu.VMEM(legendre.shape, jnp.bfloat16),
        pltpu.SemaphoreType.DMA((len(chunks),)),
        pltpu.VMEM((plan.groups, wide, plan.depth), jnp.bfloat16),
        pltpu.VMEM((plan.groups, 4, plan.block, BLK), jnp.float32),
        pltpu.VMEM((plan.groups * size, wide), jnp.float32),
        pltpu.VMEM((plan.rows, BLK), jnp.float32),
        pltpu.VMEM((waves, plan.rows, plan.lanes), jnp.float32),
        pltpu.VMEM((2, plan.rows, plan.lanes), jnp.float32),
        pltpu.VMEM((plan.rows, plan.lanes), jnp.float32),
        pltpu.VMEM((plan.hf, plan.lanes), jnp.float32),
        pltpu.VMEM((2 * plan.lanes, plan.depth), jnp.bfloat16),
        pltpu.VMEM((4, plan.images, plan.depth), jnp.float32),
        pltpu.VMEM((BLK, BLK), jnp.bfloat16),
        pltpu.VMEM((size, wide), jnp.float32),
        pltpu.VMEM((2 * wide, plan.lanes), jnp.bfloat16),
        pltpu.VMEM((size, plan.lanes), jnp.float32),
    ]
    for _, count in chunks:
        scratch += chunk_scratch(count, pack, span * pack, lat_count, lev_count)
    product = pl.pallas_call(
        functools.partial(round_trip_kernel, plan, pack, chunks),
        out_shape=jax.ShapeDtypeStruct((slots, 2 * fields, local_cols), jnp.float32),
        in_specs=[smem, smem, vmem, pl.BlockSpec(memory_space=pl.ANY), vmem],
        out_specs=vmem,
        scratch_shapes=scratch,
        compiler_params=pltpu.CompilerParams(collective_id=0, has_side_effects=True),
    )(circle_lengths, deal_list, spec_in, legendre, mixing)
    return product.reshape(slots, 2, fields, local_cols)


def solution(mesh):
    return jax.shard_map(
        local,
        mesh=mesh,
        in_specs=(
            P("lat", None, None, "lev"),
            P("lat", "lev", None),
            P("lat", None, None),
            P(),
            P(),
            P(),
        ),
        out_specs=P("lat", None, None, "lev"),
        check_vma=False,
    )
```

time: 49.9 us -> 42.9 us (0.86)
  Pallas kernels: 46.7 us -> 41.3 us
  local copies, waits for them, and re-layouts: 2.76 us -> 1.42 us
    pallas_call x3 -> x1, Pallas kernels: 46.7 us -> 41.3 us  [local(): pl.pallas_call(functools.partial(round_trip_kernel, plan, pack, chunks),...]
    unnamed x2 -> x1, local copies, waits for them, and re-layouts: 2.76 us -> 1.42 us
where the time goes in v2:
time: 42.9 us; the launch traced here: 42.7 us
  Pallas kernels  41.3 us (96%)
  local copies, waits for them, and re-layouts  1.42 us (3%)
    pallas_call x1, Pallas kernels, local(): pl.pallas_call(functools.partial(round_trip_kernel, plan, pack, chunks),...  41.3 us
    unnamed x1, local copies, waits for them, and re-layouts  1.42 us

profile of v2, /device:TPU:0, one launch (start us, length us, event | category | flops | bytes accessed | tf_op | source)
XLA Modules:
  0.0 42.7 jit_solution(17908414538536268983)
XLA Ops:
  0.0 41.3 %shard_map.55 = f32[2,16,320]{2,1,0:T(8,128)} custom-call(s32[2560]{0:T(1024)} %lengths.1, s32[8]{0:T(128)} %deal.1, bf16[2,2,8,320]{3,2,1,0:T(8,128)(2,1)} %spec_ref.1, bf16[2,320,2560]{2,1,0:T(8,128)(2,1)} %legendre_ref.1, bf16[8,8]{1,0:T(8,128)(2,1)} %mixing_ref.1), custom_call_target="tpu_custom_call" | custom-call | tf_op jit(solution)/shard_map/pallas_call | solution.py:583
  41.3 1.4 %copy.7 = f32[2,2,8,320]{3,2,1,0:T(8,128)} copy(f32[2,2,8,320]{3,2,1,0:T(8,128)} %bitcast.1) | data formatting | bytes 81920

commit v3 on v2

--- a/solution.py
+++ b/solution.py
@@ -12,7 +12,8 @@
 SPAN = 2 * BLK
 ACROSS = (((1,), (1,)), ((), ()))
 STREAMS = 2
-SPLIT = (3, 3)
+SPLIT = ((8, 10), (0, 6), (6, 8))
+DIRECT = 64
 
 
 def iota(shape, axis):
@@ -52,14 +53,9 @@
         least = pack
         while least * self.devices % (pack * BLK) or least % self.share:
             least += pack
-        units, out = self.rows // least, []
-        first = self.rows
-        for tenths in SPLIT:
-            count = units * tenths // 10 * least
-            if 0 < count < first:
-                first -= count
-                out.append((first, count))
-        return out + [(0, first)]
+        units = self.rows // least
+        marks = [(units * start // 10 * least, units * stop // 10 * least) for start, stop in SPLIT]
+        return [(start, stop - start) for start, stop in marks if stop > start]
 
 
 def waves_at(deal, index, waves):
@@ -304,16 +300,39 @@
     pl.semaphore_wait(pltpu.get_barrier_semaphore(), total)
 
 
-def hail():
+def others(count):
+    lat_count = lax.axis_size("lat")
+    me = lax.axis_index("lev") * lat_count + lax.axis_index("lat")
+    for off in range(1, count):
+        peer = lax.rem(me + off, count)
+        yield {"lat": lax.rem(peer, lat_count), "lev": lax.div(peer, lat_count)}
+
+
+def hail(direct):
     barrier = pltpu.get_barrier_semaphore()
-    total = 0
-    for axis in ("lat", "lev"):
-        for peer in peers_of(axis):
-            pl.semaphore_signal(
-                barrier, inc=1, device_id={axis: peer}, device_id_type=pl.DeviceIdType.MESH
-            )
-            total += 1
-    return total
+    if direct:
+        peers = list(others(lax.axis_size("lat") * lax.axis_size("lev")))
+    else:
+        peers = [{axis: peer} for axis in ("lat", "lev") for peer in peers_of(axis)]
+    for peer in peers:
+        pl.semaphore_signal(barrier, inc=1, device_id=peer, device_id_type=pl.DeviceIdType.MESH)
+    return len(peers)
+
+
+def send_all(sources, target, sems):
+    copies = []
+    for step, peer in enumerate(others(lax.axis_size("lat") * lax.axis_size("lev"))):
+        copy = pltpu.make_async_remote_copy(
+            src_ref=sources(peer["lev"], peer["lat"]),
+            dst_ref=target,
+            send_sem=sems.at[0, step],
+            recv_sem=sems.at[1, step],
+            device_id=peer,
+            device_id_type=pl.DeviceIdType.MESH,
+        )
+        copy.start()
+        copies.append(copy)
+    return copies
 
 
 def send(axis, sources, target, sems):
@@ -361,9 +380,9 @@
 
 def round_trip_kernel(plan, pack, chunks, lengths, deal, spec_ref, legendre_ref, mixing_ref, out_ref, *scratch):
     held, load_sems, left, table, total, row_length, products, weights, values_ref = scratch[:9]
-    keep, gather, placed_sign, mixer, sum_sign, spread, fold_keep = scratch[9:16]
+    keep, gather, placed_sign, mixer, sum_sign, spread, fold_keep, direct_sems = scratch[9:17]
     buffers = [
-        scratch[16 + at * CHUNK_REFS : 16 + (at + 1) * CHUNK_REFS] for at in range(len(chunks))
+        scratch[17 + at * CHUNK_REFS : 17 + (at + 1) * CHUNK_REFS] for at in range(len(chunks))
     ]
     slots, local_cols, half_lat = held.shape
     fields, devices = plan.fields, plan.devices
@@ -374,6 +393,8 @@
     part_span = slots * part_width
     width = part_span * pack
     faces = width // BLK
+    last = len(chunks) - 1
+    direct = devices <= DIRECT
     loads = []
     for at, (first, count) in enumerate(chunks):
         columns = pl.ds(first * devices, count * devices)
@@ -382,7 +403,7 @@
         )
         load.start()
         loads.append(load)
-    greetings = hail()
+    greetings = hail(direct)
     odd, masks = column_masks(plan, deal, slots, local_cols)
     lefts = []
     for slot in range(slots):
@@ -390,9 +411,12 @@
         kept = kept * masks[slot]
         lefts.append(jnp.concatenate([kept, kept * odd], axis=0).astype(jnp.bfloat16))
 
-    sent = []
-    for at, (first, count) in enumerate(chunks):
-        leaving, arriving, turned, lev_sems = (buffers[at][n] for n in (0, 1, 7, 8))
+    finished = []
+    reduced, crossed, returned, shared = {}, {}, {}, {}
+
+    def project(at):
+        first, count = chunks[at]
+        leaving, turned = buffers[at][0], buffers[at][7]
         each = count // pack
         loads[at].wait()
         sums = [
@@ -419,19 +443,24 @@
                 leaving[target // lat_count, target % lat_count, :, face * BLK : (face + 1) * BLK] = (
                     turned[face, pl.ds(target, each, stride=devices), :].astype(jnp.bfloat16)
                 )
-        if at == 0:
-            expect(greetings)
-        sent.append(send("lev", lambda peer, leaving=leaving: leaving.at[peer], arriving.at[lev_index], lev_sems.at[0]))
-    finished = list(sent)
-
-    fill_constants(plan, deal, mixing_ref, keep, gather, placed_sign, mixer, sum_sign, spread, fold_keep)
-    fill_tables(plan, device, lengths, deal, table, row_length)
-
-    crossed = []
-    for at, (first, count) in enumerate(chunks):
+
+    def start_reduce(at):
+        leaving, arriving, lev_sems = (buffers[at][n] for n in (0, 1, 8))
+        if at == 0 and direct:
+            copies = send_all(
+                lambda lev, lat: leaving.at[lev, lat], arriving.at[lev_index, lat_index], direct_sems.at[0]
+            )
+            arriving[lev_index, lat_index] = leaving[lev_index, lat_index]
+        else:
+            copies = send("lev", lambda peer: leaving.at[peer], arriving.at[lev_index], lev_sems.at[0])
+        reduced[at] = copies
+        finished.append(copies)
+
+    def start_cross(at):
+        count = chunks[at][1]
         arriving, summed, landed, turned, lat_sems = (buffers[at][n] for n in (1, 2, 3, 7, 9))
         each = count // pack
-        sum_of = jnp.stack(
+        total_of = jnp.stack(
             [
                 jnp.concatenate(
                     [
@@ -443,34 +472,74 @@
                 for side in range(lat_count)
             ]
         )
-        for peer in arrivals("lev", sent[at]):
-            sum_of = sum_of + arriving[peer].astype(jnp.float32)
-        summed[...] = sum_of.astype(jnp.bfloat16)
-        crossed.append(
-            send("lat", lambda peer, summed=summed: summed.at[peer], landed.at[lat_index], lat_sems.at[0])
-        )
+        for peer in arrivals("lev", reduced[at]):
+            total_of = total_of + arriving[peer].astype(jnp.float32)
+        summed[...] = total_of.astype(jnp.bfloat16)
+        crossed[at] = send("lat", lambda peer: summed.at[peer], landed.at[lat_index], lat_sems.at[0])
         landed[lat_index] = summed[lat_index]
-        if at == 0:
-            fill_products(plan, device, row_length, deal, products, weights)
-    finished += crossed
-
-    returned, shared = [], []
+        finished.append(crossed[at])
+
+    def land(at):
+        arriving, landed = buffers[at][1], buffers[at][3]
+        if at == 0 and direct:
+            for copy in reduced[at]:
+                copy.wait_recv()
+            blocks = []
+            for side in range(lat_count):
+                block = arriving[0, side].astype(jnp.float32)
+                for lev in range(1, lev_count):
+                    block = block + arriving[lev, side].astype(jnp.float32)
+                blocks.append(block.astype(jnp.bfloat16).astype(jnp.float32))
+            return blocks
+        for _ in arrivals("lat", crossed[at]):
+            pass
+        return [landed[side].astype(jnp.float32) for side in range(lat_count)]
+
+    def start_return(at):
+        rows, back, gathered, lat_sems = (buffers[at][n] for n in (4, 5, 6, 9))
+        if at == last and direct:
+            shared[at] = send_all(
+                lambda lev, lat: rows.at[lat], gathered.at[lev_index, lat_index], direct_sems.at[1]
+            )
+            gathered[lev_index, lat_index] = rows[lat_index]
+            finished.append(shared[at])
+        else:
+            returned[at] = send("lat", lambda peer: rows.at[peer], back.at[lat_index], lat_sems.at[1])
+            back[lat_index] = rows[lat_index]
+            finished.append(returned[at])
 
     def pass_on(at):
+        if at in shared:
+            return
         back, gathered, lev_sems = (buffers[at][n] for n in (5, 6, 8))
         for _ in arrivals("lat", returned[at]):
             pass
-        copies = send("lev", lambda peer: back, gathered.at[lev_index], lev_sems.at[1])
+        shared[at] = send("lev", lambda peer: back, gathered.at[lev_index], lev_sems.at[1])
         gathered[lev_index] = back[...]
-        shared.append(copies)
-        finished.append(copies)
+        finished.append(shared[at])
+
+    project(0)
+    expect(greetings)
+    start_reduce(0)
+    if last > 0:
+        project(1)
+        start_reduce(1)
+    for at in range(2, len(chunks)):
+        project(at)
+    fill_constants(plan, deal, mixing_ref, keep, gather, placed_sign, mixer, sum_sign, spread, fold_keep)
+    fill_tables(plan, device, lengths, deal, table, row_length)
+    if not direct:
+        start_cross(0)
+    if last > 0:
+        start_cross(1)
+    if last > 1:
+        start_reduce(2)
+    fill_products(plan, device, row_length, deal, products, weights)
 
     for at, (first, count) in enumerate(chunks):
-        landed, leaving_rows, back, lat_sems = (buffers[at][n] for n in (3, 4, 5, 9))
+        rows = buffers[at][4]
         each = count // pack
-        for _ in arrivals("lat", crossed[at]):
-            pass
-        blocks = [landed[side].astype(jnp.float32) for side in range(lat_count)]
+        blocks = land(at)
         values = jnp.concatenate(
             [
                 jnp.concatenate(
@@ -484,13 +553,9 @@
         values_ref[first : first + count] = values
         place_coefficients(plan, first, values, keep, gather, placed_sign, mixer, left)
         groups = list(range(first // plan.share, (first + count) // plan.share))
-        if at:
-            middle = len(groups) // 2
-            walk_circles(plan, groups[middle:], device, lengths, table, left, total)
+        walk_circles(plan, groups, device, lengths, table, left, total)
+        if 0 < at < last:
             pass_on(at - 1)
-            groups = groups[:middle]
-        if groups:
-            walk_circles(plan, groups, device, lengths, table, left, total)
         size = 2 * plan.block
         result = fold_circles(
             plan,
@@ -504,27 +569,28 @@
             result = result + products[other, first : first + count] * rolled(plan, values, other)
         result = result * weights[1, first : first + count]
         for side in range(lat_count):
-            leaving_rows[side] = jnp.concatenate(
+            rows[side] = jnp.concatenate(
                 [
                     result[part * each : (part + 1) * each, side * part_span : (side + 1) * part_span]
                     for part in range(pack)
                 ],
                 axis=1,
             ).astype(jnp.bfloat16)
-        returned.append(
-            send("lat", lambda peer, rows=leaving_rows: rows.at[peer], back.at[lat_index], lat_sems.at[1])
-        )
-        back[lat_index] = leaving_rows[lat_index]
-    finished += returned
+        start_return(at)
+        if at + 2 <= last:
+            start_cross(at + 2)
+            if at + 3 <= last:
+                start_reduce(at + 3)
+    if last > 0:
+        pass_on(last - 1)
 
     sums = [None] * slots
     for at, (first, count) in enumerate(chunks):
         gathered, turned = buffers[at][6], buffers[at][7]
         each = count // pack
-        if at == len(chunks) - 1:
-            pass_on(at)
-        for _ in arrivals("lev", shared[at]):
-            pass
+        pass_on(at)
+        for copy in shared[at]:
+            copy.wait_recv()
         for source in range(devices):
             block = gathered[source // lat_count, source % lat_count].astype(jnp.float32)
             for face in range(faces):
@@ -577,6 +643,7 @@
         pltpu.VMEM((size, wide), jnp.float32),
         pltpu.VMEM((2 * wide, plan.lanes), jnp.bfloat16),
         pltpu.VMEM((size, plan.lanes), jnp.float32),
+        pltpu.SemaphoreType.DMA((2, 2, min(plan.devices, DIRECT))),
     ]
     for _, count in chunks:
         scratch += chunk_scratch(count, pack, span * pack, lat_count, lev_count)

time: 42.9 us -> 37.3 us (0.87)
  Pallas kernels: 41.3 us -> 35.7 us
    pallas_call x1, Pallas kernels: 41.3 us -> 35.7 us  [local(): pl.pallas_call(functools.partial(round_trip_kernel, plan, pack, chunks),...]
where the time goes in v3:
time: 37.3 us; the launch traced here: 37.1 us
  Pallas kernels  35.7 us (96%)
  local copies, waits for them, and re-layouts  1.42 us (4%)
    pallas_call x1, Pallas kernels, local(): pl.pallas_call(functools.partial(round_trip_kernel, plan, pack, chunks),...  35.7 us
    unnamed x1, local copies, waits for them, and re-layouts  1.42 us

profile of v3, /device:TPU:0, one launch (start us, length us, event | category | flops | bytes accessed | tf_op | source)
XLA Modules:
  0.0 37.1 jit_solution(1874465395028531417)
XLA Ops:
  0.0 35.7 %shard_map.55 = f32[2,16,320]{2,1,0:T(8,128)} custom-call(s32[2560]{0:T(1024)} %lengths.1, s32[8]{0:T(128)} %deal.1, bf16[2,2,8,320]{3,2,1,0:T(8,128)(2,1)} %spec_ref.1, bf16[2,320,2560]{2,1,0:T(8,128)(2,1)} %legendre_ref.1, bf16[8,8]{1,0:T(8,128)(2,1)} %mixing_ref.1), custom_call_target="tpu_custom_call" | custom-call | tf_op jit(solution)/shard_map/pallas_call | solution.py:650
  35.7 1.4 %copy.7 = f32[2,2,8,320]{3,2,1,0:T(8,128)} copy(f32[2,2,8,320]{3,2,1,0:T(8,128)} %bitcast.1) | data formatting | bytes 81920

commit v4 on v3

--- a/solution.py
+++ b/solution.py
@@ -11,7 +11,7 @@
 BLK = 128
 SPAN = 2 * BLK
 ACROSS = (((1,), (1,)), ((), ()))
-STREAMS = 2
+STREAMS = 4
 SPLIT = ((8, 10), (0, 6), (6, 8))
 DIRECT = 64
 
@@ -42,12 +42,15 @@
         self.scale = (2.0 * waves) ** (-0.5)
 
     def tiles(self, group):
-        last = ((group + 1) * self.share - 1) * self.devices + self.devices - 1
-        return -(-(last + 6) // SPAN)
-
-    def inside(self, group, tile):
+        needed = (group + 1) * self.share * self.devices + 5
+        tiles = [(at, SPAN) for at in range(0, needed, SPAN)]
+        if needed - tiles[-1][0] <= BLK:
+            tiles[-1] = tiles[-1][0], BLK
+        return tiles
+
+    def inside(self, group, at, span):
         first = group * self.share * self.devices
-        return (tile + 1) * SPAN - 1 < 3 + first - first // 2
+        return at > 0 and at + span - 1 < 3 + first - first // 2
 
     def chunks(self, pack):
         least = pack
@@ -65,29 +68,50 @@
     return out
 
 
+def circle_point(turns):
+    quadrant = jnp.floor(4.0 * turns + 0.5)
+    angle = (turns - 0.25 * quadrant) * (2.0 * math.pi)
+    square = angle * angle
+    sine = angle * (
+        1.0 + square * (-1.0 / 6 + square * (1.0 / 120 + square * (-1.0 / 5040 + square * (1.0 / 362880))))
+    )
+    cosine = 1.0 + square * (
+        -0.5 + square * (1.0 / 24 + square * (-1.0 / 720 + square * (1.0 / 40320 - square * (1.0 / 3628800))))
+    )
+    turned = (quadrant == 1.0) | (quadrant == 3.0)
+    first, second = jnp.where(turned, sine, cosine), jnp.where(turned, cosine, sine)
+    first = jnp.where((quadrant == 1.0) | (quadrant == 2.0), -first, first)
+    second = jnp.where((quadrant == 2.0) | (quadrant == 3.0), -second, second)
+    return first, second
+
+
 def fill_tables(plan, device, lengths, deal, table, row_length):
     wave = waves_at(deal, iota((plan.block, BLK), 0) % plan.waves, plan.waves).astype(jnp.float32)
     product = wave * iota((plan.block, BLK), 1).astype(jnp.float32)
-    member = iota((plan.block, 1), 0) // plan.waves
-
-    def fill(group, carry):
-        length = jnp.zeros((plan.block, 1), jnp.float32)
-        for each in range(plan.share):
-            own = lengths[(group * plan.share + each) * plan.devices + device].astype(jnp.float32)
-            length = jnp.where(member == each, own, length)
-            row_length[pl.ds(group * plan.share + each, 1), :] = jnp.full((1, BLK), own, jnp.float32)
-        turned = product - jnp.floor(product / length) * length
-        angle = turned * (2.0 * math.pi) / length
-        cosine, sine = jnp.cos(angle), jnp.sin(angle)
-        last_cos, last_sin = cosine[:, BLK - 1 : BLK], sine[:, BLK - 1 : BLK]
-        next_cos, next_sin = cosine[:, 1:2], sine[:, 1:2]
-        table[group, 0] = cosine
-        table[group, 1] = -sine
-        table[group, 2] = jnp.broadcast_to(last_cos * next_cos - last_sin * next_sin, product.shape)
-        table[group, 3] = jnp.broadcast_to(-last_sin * next_cos - last_cos * next_sin, product.shape)
+    member = iota((plan.block, BLK), 0) // plan.waves
+    unroll = max(n for n in range(1, 6) if plan.groups % n == 0)
+
+    def fill(step, carry):
+        for near in range(unroll):
+            group = step * unroll + near
+            length = jnp.zeros((plan.block, BLK), jnp.float32)
+            for each in range(plan.share):
+                own = lengths[(group * plan.share + each) * plan.devices + device].astype(jnp.float32)
+                length = jnp.where(member == each, own, length)
+                row_length[pl.ds(group * plan.share + each, 1), :] = jnp.full((1, BLK), own, jnp.float32)
+            inverse = 1.0 / length
+            turned = product - jnp.floor(product * inverse) * length
+            cosine, sine = circle_point(turned * inverse)
+            last_cos, last_sin = cosine[:, BLK - 1 : BLK], sine[:, BLK - 1 : BLK]
+            next_cos, next_sin = cosine[:, 1:2], sine[:, 1:2]
+            table[group, 0] = cosine
+            table[group, 1] = -sine
+            table[group, 2] = jnp.broadcast_to(last_cos * next_cos - last_sin * next_sin, product.shape)
+            table[group, 3] = jnp.broadcast_to(-last_sin * next_cos - last_cos * next_sin, product.shape)
+            table[group, 4] = 0.25 * length + 0.5
         return carry
 
-    lax.fori_loop(0, plan.groups, fill, 0)
+    lax.fori_loop(0, plan.groups // unroll, fill, 0)
 
 
 def lane_waves(plan, deal):
@@ -201,14 +225,13 @@
             ] = (own * placed_sign[image]).astype(jnp.bfloat16)
 
 
-def walk_circles(plan, groups, device, lengths, table, left, total):
-    position = iota((1, SPAN), 1)
-    member = iota((plan.block, 1), 0) // plan.waves
-
-    def phases(group, tile, cos_now, sin_now):
+def walk_circles(plan, groups, table, left, total):
+    position = iota((1, SPAN), 1).astype(jnp.float32)
+
+    def phases(group, at, span, cos_now, sin_now):
         step_cos, step_sin = table[group, 2], table[group, 3]
         cosines, sines = [], []
-        for _ in range(SPAN // BLK):
+        for _ in range(span // BLK):
             cosines.append(cos_now)
             sines.append(sin_now)
             cos_now, sin_now = (
@@ -218,22 +241,18 @@
         cosine, sine = jnp.concatenate(cosines, axis=1), jnp.concatenate(sines, axis=1)
         near, far = cosine.astype(jnp.bfloat16), sine.astype(jnp.bfloat16)
         weights = jnp.concatenate([near, far, near, far], axis=0)
-        if tile > 0 and plan.inside(group, tile):
+        if plan.inside(group, at, span):
             return cos_now, sin_now, weights, weights[: 2 * plan.block]
-        at = position + tile * SPAN
-        quarter = jnp.zeros((plan.block, 1), jnp.int32)
-        for each in range(plan.share):
-            own = lengths[(group * plan.share + each) * plan.devices + device]
-            quarter = jnp.where(member == each, lax.shift_right_logical(own, 2), quarter)
-        share = jnp.where(at < quarter, 1.0, jnp.where(at == quarter, 0.5, 0.0)).astype(jnp.float32)
-        if tile == 0:
-            share = share * jnp.where(at == 0, 0.5, 1.0).astype(jnp.float32)
+        limit = jnp.concatenate([table[group, 4]] * (span // BLK), axis=1)
+        share = jnp.clip(limit - (position[:, :span] + float(at)), 0.0, 1.0)
+        if at == 0:
+            share = share * jnp.where(position[:, :span] == 0.0, 0.5, 1.0)
         shared = jnp.concatenate([cosine * share, sine * share], axis=0).astype(jnp.bfloat16)
         return cos_now, sin_now, weights, shared
 
     streams = [[] for _ in range(STREAMS)]
-    for group in sorted(groups, key=lambda group: -plan.tiles(group)):
-        min(streams, key=len).extend((group, tile) for tile in range(plan.tiles(group)))
+    for group in sorted(groups, key=lambda group: -len(plan.tiles(group))):
+        min(streams, key=len).extend((group, at, span) for at, span in plan.tiles(group))
     state, sums, waiting = {}, {}, []
 
     def finish():
@@ -251,10 +270,10 @@
         started = []
         for stream in streams:
             if step < len(stream):
-                group, tile = stream[step]
+                group, at, span = stream[step]
                 if group not in state:
                     state[group] = table[group, 0], table[group, 1]
-                cos_now, sin_now, weights, shared = phases(group, tile, *state[group])
+                cos_now, sin_now, weights, shared = phases(group, at, span, *state[group])
                 state[group] = cos_now, sin_now
                 grid = jnp.dot(left[group], weights, preferred_element_type=jnp.float32)
                 started.append((group, shared, grid))
@@ -378,11 +397,14 @@
 CHUNK_REFS = 10
 
 
-def round_trip_kernel(plan, pack, chunks, lengths, deal, spec_ref, legendre_ref, mixing_ref, out_ref, *scratch):
+def round_trip_kernel(
+    plan, pack, chunks, lengths_in, deal_in, spec_in, legendre_ref, mixing_in, out_ref, *scratch
+):
     held, load_sems, left, table, total, row_length, products, weights, values_ref = scratch[:9]
     keep, gather, placed_sign, mixer, sum_sign, spread, fold_keep, direct_sems = scratch[9:17]
+    lengths, deal, spec_ref, mixing_ref, input_sems = scratch[17:22]
     buffers = [
-        scratch[17 + at * CHUNK_REFS : 17 + (at + 1) * CHUNK_REFS] for at in range(len(chunks))
+        scratch[22 + at * CHUNK_REFS : 22 + (at + 1) * CHUNK_REFS] for at in range(len(chunks))
     ]
     slots, local_cols, half_lat = held.shape
     fields, devices = plan.fields, plan.devices
@@ -395,6 +417,15 @@
     faces = width // BLK
     last = len(chunks) - 1
     direct = devices <= DIRECT
+    greetings = hail(direct)
+    inputs = [
+        pltpu.make_async_copy(source, target, input_sems.at[at])
+        for at, (source, target) in enumerate(
+            ((deal_in, deal), (spec_in, spec_ref), (lengths_in, lengths), (mixing_in, mixing_ref))
+        )
+    ]
+    for load in inputs:
+        load.start()
     loads = []
     for at, (first, count) in enumerate(chunks):
         columns = pl.ds(first * devices, count * devices)
@@ -403,7 +434,8 @@
         )
         load.start()
         loads.append(load)
-    greetings = hail(direct)
+    inputs[0].wait()
+    inputs[1].wait()
     odd, masks = column_masks(plan, deal, slots, local_cols)
     lefts = []
     for slot in range(slots):
@@ -519,6 +551,10 @@
         finished.append(shared[at])
 
     project(0)
+    inputs[2].wait()
+    inputs[3].wait()
+    fill_constants(plan, deal, mixing_ref, keep, gather, placed_sign, mixer, sum_sign, spread, fold_keep)
+    fill_tables(plan, device, lengths, deal, table, row_length)
     expect(greetings)
     start_reduce(0)
     if last > 0:
@@ -526,8 +562,6 @@
         start_reduce(1)
     for at in range(2, len(chunks)):
         project(at)
-    fill_constants(plan, deal, mixing_ref, keep, gather, placed_sign, mixer, sum_sign, spread, fold_keep)
-    fill_tables(plan, device, lengths, deal, table, row_length)
     if not direct:
         start_cross(0)
     if last > 0:
@@ -553,7 +587,7 @@
         values_ref[first : first + count] = values
         place_coefficients(plan, first, values, keep, gather, placed_sign, mixer, left)
         groups = list(range(first // plan.share, (first + count) // plan.share))
-        walk_circles(plan, groups, device, lengths, table, left, total)
+        walk_circles(plan, groups, table, left, total)
         if 0 < at < last:
             pass_on(at - 1)
         size = 2 * plan.block
@@ -624,13 +658,12 @@
     pack = max(1, BLK // span)
     chunks = plan.chunks(pack)
     vmem = pl.BlockSpec(memory_space=pltpu.VMEM)
-    smem = pl.BlockSpec(memory_space=pltpu.SMEM)
     size, wide = 2 * plan.block, 4 * plan.images
     scratch = [
         pltpu.VMEM(legendre.shape, jnp.bfloat16),
         pltpu.SemaphoreType.DMA((len(chunks),)),
         pltpu.VMEM((plan.groups, wide, plan.depth), jnp.bfloat16),
-        pltpu.VMEM((plan.groups, 4, plan.block, BLK), jnp.float32),
+        pltpu.VMEM((plan.groups, 5, plan.block, BLK), jnp.float32),
         pltpu.VMEM((plan.groups * size, wide), jnp.float32),
         pltpu.VMEM((plan.rows, BLK), jnp.float32),
         pltpu.VMEM((waves, plan.rows, plan.lanes), jnp.float32),
@@ -644,13 +677,18 @@
         pltpu.VMEM((2 * wide, plan.lanes), jnp.bfloat16),
         pltpu.VMEM((size, plan.lanes), jnp.float32),
         pltpu.SemaphoreType.DMA((2, 2, min(plan.devices, DIRECT))),
+        pltpu.SMEM(circle_lengths.shape, jnp.int32),
+        pltpu.SMEM(deal_list.shape, jnp.int32),
+        pltpu.VMEM(spec_in.shape, jnp.bfloat16),
+        pltpu.VMEM(mixing.shape, jnp.bfloat16),
+        pltpu.SemaphoreType.DMA((4,)),
     ]
     for _, count in chunks:
         scratch += chunk_scratch(count, pack, span * pack, lat_count, lev_count)
     product = pl.pallas_call(
         functools.partial(round_trip_kernel, plan, pack, chunks),
         out_shape=jax.ShapeDtypeStruct((slots, 2 * fields, local_cols), jnp.float32),
-        in_specs=[smem, smem, vmem, pl.BlockSpec(memory_space=pl.ANY), vmem],
+        in_specs=[pl.BlockSpec(memory_space=pl.ANY)] * 5,
         out_specs=vmem,
         scratch_shapes=scratch,
         compiler_params=pltpu.CompilerParams(collective_id=0, has_side_effects=True),

time: 37.3 us -> 34.8 us (0.933)
  Pallas kernels: 35.7 us -> 33.2 us
    pallas_call x1, Pallas kernels: 35.7 us -> 33.2 us  [local(): pl.pallas_call(functools.partial(round_trip_kernel, plan, pack, chunks),...]
where the time goes in v4:
time: 34.8 us; the launch traced here: 34.7 us
  Pallas kernels  33.2 us (95%)
  local copies, waits for them, and re-layouts  1.42 us (4%)
    pallas_call x1, Pallas kernels, local(): pl.pallas_call(functools.partial(round_trip_kernel, plan, pack, chunks),...  33.2 us
    unnamed x1, local copies, waits for them, and re-layouts  1.42 us

profile of v4, /device:TPU:0, one launch (start us, length us, event | category | flops | bytes accessed | tf_op | source)
XLA Modules:
  0.0 34.7 jit_solution(11998488151870402020)
XLA Ops:
  0.0 33.2 %shard_map.55 = f32[2,16,320]{2,1,0:T(8,128)} custom-call(s32[2560]{0:T(1024)} %lengths_in.1, s32[8]{0:T(128)} %deal_in.1, bf16[2,2,8,320]{3,2,1,0:T(8,128)(2,1)} %spec_in.1, bf16[2,320,2560]{2,1,0:T(8,128)(2,1)} %legendre_ref.1, bf16[8,8]{1,0:T(8,128)(2,1)} %mixing_in.1), custom_call_target="tpu_custom_call" | custom-call | tf_op jit(solution)/shard_map/pallas_call | solution.py:688
  33.2 1.4 %copy.7 = f32[2,2,8,320]{3,2,1,0:T(8,128)} copy(f32[2,2,8,320]{3,2,1,0:T(8,128)} %bitcast.1) | data formatting | bytes 81920

commit v5 on v4

--- a/solution.py
+++ b/solution.py
@@ -11,8 +11,8 @@
 BLK = 128
 SPAN = 2 * BLK
 ACROSS = (((1,), (1,)), ((), ()))
-STREAMS = 4
-SPLIT = ((8, 10), (0, 6), (6, 8))
+STREAMS = 2
+SPLIT = ((8, 10), (0, 4), (4, 8))
 DIRECT = 64
 
 
@@ -39,6 +39,8 @@
         self.block = self.share * waves
         self.depth = 4 * self.block
         self.images = self.share * self.hf
+        self.own = 4 * self.hf
+        self.face = max(BLK, self.own)
         self.scale = (2.0 * waves) ** (-0.5)
 
     def tiles(self, group):
@@ -159,19 +161,21 @@
     mixer[...] = jnp.where(same, whole, 0.0).astype(jnp.bfloat16)
     size, wide = sum_sign.shape
     down, right = iota((size, wide), 0), iota((size, wide), 1)
+    each = down // (2 * waves)
+    lane = each * plan.own // plan.face * plan.face + right
     odd = waves_at(deal, down % waves, waves) % 2 == 1
-    sine = down // plan.block == 1
+    sine = down // waves % 2 == 1
     sign = jnp.zeros((size, wide), jnp.float32)
     for image in range(4):
-        sign = jnp.where(right // plan.images == image, image_sign(image, sine, odd), sign)
-    sum_sign[...] = sign * unit(down % plan.block // waves == right % plan.images // hf)
+        sign = jnp.where(lane % plan.own // hf == image, image_sign(image, sine, odd), sign)
+    sum_sign[...] = sign * unit(each == lane // plan.own)
     down, right = iota((2 * wide, lanes), 0), iota((2 * wide, lanes), 1)
     spread[...] = unit(
         down % hf == right // (2 * fields) % 2 * fields + right % fields
     ).astype(jnp.bfloat16)
     down, right = iota((size, lanes), 0), iota((size, lanes), 1)
     fold_keep[...] = unit(
-        (down // plan.block == right // fields % 2) & (down % waves == right // (4 * fields))
+        (down // waves % 2 == right // fields % 2) & (down % waves == right // (4 * fields))
     )
 
 
@@ -218,11 +222,13 @@
     )
     placed = jnp.dot(spread, gather[...], preferred_element_type=jnp.float32)
     for group in range(rows // plan.share):
-        own = placed[group * plan.images : (group + 1) * plan.images]
-        for image in range(4):
-            left[
-                first // plan.share + group, image * plan.images : (image + 1) * plan.images, :
-            ] = (own * placed_sign[image]).astype(jnp.bfloat16)
+        for each in range(plan.share):
+            at = (group * plan.share + each) * plan.hf
+            for image in range(4):
+                to = each * plan.own + image * plan.hf
+                left[first // plan.share + group, to : to + plan.hf, :] = (
+                    placed[at : at + plan.hf] * placed_sign[image, each * plan.hf : (each + 1) * plan.hf, :]
+                ).astype(jnp.bfloat16)
 
 
 def walk_circles(plan, groups, table, left, total):
@@ -263,7 +269,14 @@
                 ACROSS,
                 preferred_element_type=jnp.float32,
             )
-            sums[group] = sums[group] + extra if group in sums else extra
+            parts = []
+            for each in range(plan.share):
+                side = each * plan.own // plan.face * plan.face
+                for row in (each * plan.waves, plan.block + each * plan.waves):
+                    parts.append(extra[row : row + plan.waves, side : side + plan.face])
+            if group in sums:
+                parts = [old + new for old, new in zip(sums[group], parts)]
+            sums[group] = parts
         waiting.clear()
 
     for step in range(max(len(stream) for stream in streams)):
@@ -282,7 +295,8 @@
     finish()
     size = 2 * plan.block
     for group in groups:
-        total[group * size : (group + 1) * size, :] = sums[group]
+        for at, part in enumerate(sums[group]):
+            total[group * size + at * plan.waves : group * size + (at + 1) * plan.waves, :] = part
 
 
 def fold_circles(plan, sums, sum_sign, spread, fold_keep):
@@ -295,9 +309,9 @@
         jnp.concatenate([high, low], axis=1), spread[...], preferred_element_type=jnp.float32
     )
     kept = (folded.reshape(count, size, plan.lanes) * fold_keep[...][None]).reshape(
-        count, 2, plan.share, plan.waves, plan.lanes
+        count * plan.share, 2, plan.waves, plan.lanes
     )
-    return jnp.sum(jnp.sum(kept, axis=1), axis=2).reshape(count * plan.share, plan.lanes)
+    return jnp.sum(jnp.sum(kept, axis=1), axis=1)
 
 
 def column_masks(plan, deal, slots, local_cols):
@@ -659,12 +673,13 @@
     chunks = plan.chunks(pack)
     vmem = pl.BlockSpec(memory_space=pltpu.VMEM)
     size, wide = 2 * plan.block, 4 * plan.images
+    face = plan.face
     scratch = [
         pltpu.VMEM(legendre.shape, jnp.bfloat16),
         pltpu.SemaphoreType.DMA((len(chunks),)),
         pltpu.VMEM((plan.groups, wide, plan.depth), jnp.bfloat16),
         pltpu.VMEM((plan.groups, 5, plan.block, BLK), jnp.float32),
-        pltpu.VMEM((plan.groups * size, wide), jnp.float32),
+        pltpu.VMEM((plan.groups * size, face), jnp.float32),
         pltpu.VMEM((plan.rows, BLK), jnp.float32),
         pltpu.VMEM((waves, plan.rows, plan.lanes), jnp.float32),
         pltpu.VMEM((2, plan.rows, plan.lanes), jnp.float32),
@@ -673,8 +688,8 @@
         pltpu.VMEM((2 * plan.lanes, plan.depth), jnp.bfloat16),
         pltpu.VMEM((4, plan.images, plan.depth), jnp.float32),
         pltpu.VMEM((BLK, BLK), jnp.bfloat16),
-        pltpu.VMEM((size, wide), jnp.float32),
-        pltpu.VMEM((2 * wide, plan.lanes), jnp.bfloat16),
+        pltpu.VMEM((size, face), jnp.float32),
+        pltpu.VMEM((2 * face, plan.lanes), jnp.bfloat16),
         pltpu.VMEM((size, plan.lanes), jnp.float32),
         pltpu.SemaphoreType.DMA((2, 2, min(plan.devices, DIRECT))),
         pltpu.SMEM(circle_lengths.shape, jnp.int32),
@@ -688,10 +703,12 @@
     product = pl.pallas_call(
         functools.partial(round_trip_kernel, plan, pack, chunks),
         out_shape=jax.ShapeDtypeStruct((slots, 2 * fields, local_cols), jnp.float32),
-        in_specs=[pl.BlockSpec(memory_space=pl.ANY)] * 5,
+        in_specs=[pl.BlockSpec(memory_space=pltpu.HBM)] * 5,
         out_specs=vmem,
         scratch_shapes=scratch,
-        compiler_params=pltpu.CompilerParams(collective_id=0, has_side_effects=True),
+        compiler_params=pltpu.CompilerParams(
+            collective_id=0, has_side_effects=True
+        ),
     )(circle_lengths, deal_list, spec_in, legendre, mixing)
     return product.reshape(slots, 2, fields, local_cols)
 

time: 34.8 us -> 34 us (0.977)
  Pallas kernels: 33.2 us -> 32.4 us
    pallas_call x1, Pallas kernels: 33.2 us -> 32.4 us  [local(): pl.pallas_call(functools.partial(round_trip_kernel, plan, pack, chunks),...]
where the time goes in v5:
time: 34 us; the launch traced here: 33.8 us
  Pallas kernels  32.4 us (95%)
  local copies, waits for them, and re-layouts  1.42 us (4%)
    pallas_call x1, Pallas kernels, local(): pl.pallas_call(functools.partial(round_trip_kernel, plan, pack, chunks),...  32.4 us
    unnamed x1, local copies, waits for them, and re-layouts  1.42 us

profile of v5, /device:TPU:0, one launch (start us, length us, event | category | flops | bytes accessed | tf_op | source)
XLA Modules:
  0.0 33.8 jit_solution(17578706587237351980)
XLA Ops:
  0.0 32.4 %shard_map.55 = f32[2,16,320]{2,1,0:T(8,128)} custom-call(s32[2560]{0:T(1024)} %lengths_in.1, s32[8]{0:T(128)} %deal_in.1, bf16[2,2,8,320]{3,2,1,0:T(8,128)(2,1)} %spec_in.1, bf16[2,320,2560]{2,1,0:T(8,128)(2,1)} %legendre_ref.1, bf16[8,8]{1,0:T(8,128)(2,1)} %mixing_in.1), custom_call_target="tpu_custom_call" | custom-call | tf_op jit(solution)/shard_map/pallas_call | solution.py:703
  32.4 1.4 %copy.7 = f32[2,2,8,320]{3,2,1,0:T(8,128)} copy(f32[2,2,8,320]{3,2,1,0:T(8,128)} %bitcast.1) | data formatting | bytes 81920

commit v6 on v5

--- a/solution.py
+++ b/solution.py
@@ -37,7 +37,7 @@
         )
         self.groups = self.rows // self.share
         self.block = self.share * waves
-        self.depth = 4 * self.block
+        self.depth = 2 * self.block
         self.images = self.share * self.hf
         self.own = 4 * self.hf
         self.face = max(BLK, self.own)
@@ -140,9 +140,9 @@
     waves, fields, hf, lanes = plan.waves, plan.fields, plan.hf, plan.lanes
     lane = iota((hf, lanes), 1)
     keep[...] = unit(lane // (2 * fields) % 2 * fields + lane % fields == iota((hf, lanes), 0))
-    down, right = iota((2 * lanes, plan.depth), 0), iota((2 * lanes, plan.depth), 1)
-    down_kind = down // lanes * 2 + down % lanes // fields % 2
-    down_wave = down % lanes // (4 * fields)
+    down, right = iota((lanes, plan.depth), 0), iota((lanes, plan.depth), 1)
+    down_kind = down // fields % 2
+    down_wave = down // (4 * fields)
     gather[...] = unit(
         (down_kind == right // plan.block) & (down_wave == right % waves)
     ).astype(jnp.bfloat16)
@@ -212,14 +212,7 @@
         ],
         axis=1,
     )
-    high = mixed.astype(jnp.bfloat16).astype(jnp.float32)
-    spread = jnp.concatenate(
-        [
-            (source[:, None, :] * keep[...][None]).reshape(rows * plan.hf, plan.lanes).astype(jnp.bfloat16)
-            for source in (high, mixed - high)
-        ],
-        axis=1,
-    )
+    spread = (mixed[:, None, :] * keep[...][None]).reshape(rows * plan.hf, plan.lanes).astype(jnp.bfloat16)
     placed = jnp.dot(spread, gather[...], preferred_element_type=jnp.float32)
     for group in range(rows // plan.share):
         for each in range(plan.share):
@@ -246,7 +239,7 @@
             )
         cosine, sine = jnp.concatenate(cosines, axis=1), jnp.concatenate(sines, axis=1)
         near, far = cosine.astype(jnp.bfloat16), sine.astype(jnp.bfloat16)
-        weights = jnp.concatenate([near, far, near, far], axis=0)
+        weights = jnp.concatenate([near, far], axis=0)
         if plan.inside(group, at, span):
             return cos_now, sin_now, weights, weights[: 2 * plan.block]
         limit = jnp.concatenate([table[group, 4]] * (span // BLK), axis=1)
@@ -685,7 +678,7 @@
         pltpu.VMEM((2, plan.rows, plan.lanes), jnp.float32),
         pltpu.VMEM((plan.rows, plan.lanes), jnp.float32),
         pltpu.VMEM((plan.hf, plan.lanes), jnp.float32),
-        pltpu.VMEM((2 * plan.lanes, plan.depth), jnp.bfloat16),
+        pltpu.VMEM((plan.lanes, plan.depth), jnp.bfloat16),
         pltpu.VMEM((4, plan.images, plan.depth), jnp.float32),
         pltpu.VMEM((BLK, BLK), jnp.bfloat16),
         pltpu.VMEM((size, face), jnp.float32),

time: 34 us -> 34.2 us (level)
  no operation moved by 1% of the time
where the time goes in v6:
time: 34.2 us; the launch traced here: 34 us
  Pallas kernels  32.6 us (95%)
  local copies, waits for them, and re-layouts  1.42 us (4%)
    pallas_call x1, Pallas kernels, local(): pl.pallas_call(functools.partial(round_trip_kernel, plan, pack, chunks),...  32.6 us
    unnamed x1, local copies, waits for them, and re-layouts  1.42 us

profile of v6, /device:TPU:0, one launch (start us, length us, event | category | flops | bytes accessed | tf_op | source)
XLA Modules:
  0.0 34.0 jit_solution(757498775283171043)
XLA Ops:
  0.0 32.6 %shard_map.55 = f32[2,16,320]{2,1,0:T(8,128)} custom-call(s32[2560]{0:T(1024)} %lengths_in.1, s32[8]{0:T(128)} %deal_in.1, bf16[2,2,8,320]{3,2,1,0:T(8,128)(2,1)} %spec_in.1, bf16[2,320,2560]{2,1,0:T(8,128)(2,1)} %legendre_ref.1, bf16[8,8]{1,0:T(8,128)(2,1)} %mixing_in.1), custom_call_target="tpu_custom_call" | custom-call | tf_op jit(solution)/shard_map/pallas_call | solution.py:696
  32.6 1.4 %copy.7 = f32[2,2,8,320]{3,2,1,0:T(8,128)} copy(f32[2,2,8,320]{3,2,1,0:T(8,128)} %bitcast.1) | data formatting | bytes 81920
